TPU v7x, 32 devices: a whole 2x2x4 slice. The times are simulated.
32 devices in a mesh: field: 2 (over x), cap: 4 (over y, core), bank: 4 (over z).
Axes of the slice: x: 2, y: 2, z: 4, core: 2. Of those that a mesh axis runs over, the one named last changes fastest.
Arguments:
- pattern: bfloat16 [4, 3, 542, 512], P('cap', None, None, 'field'), may hold values from -6 to 6
- measured: bfloat16 [4, 3, 32, 512], P('cap', None, None, 'field'), may hold values from -6 to 6
- row_kernels: bfloat16 [4, 3, 16, 511], P('field', None, 'bank'), may hold values from -0.125 to 0.125
- col_kernels: bfloat16 [4, 3, 16, 511], P('field', None, 'bank'), may hold values from -0.125 to 0.125
- tile_patch: int32 [4], P('field'), may hold values from 0 to 1
- sat_tiles: int32 [4, 256], P('cap'), may hold values from 0 to 63
Outputs:
- grad_rows: float32 [4, 3, 16, 511], P('field', None, 'bank')
- grad_cols: float32 [4, 3, 16, 511], P('field', None, 'bank')
Inputs may be any that keep to these rules, and one draw needn't show every extreme that they name: Patch t of the window uses kernel set (t // 2) * 2 + tile_patch[t]. `sat_tiles`: tile numbers run row by row over tiles of 16 x 16 pixels of the window; an entry may repeat.
All inputs are finite; a program needn't handle non-finite values.
Results may differ from a plain program's by a relative error of at most 0.0033.
Values may be sent and summed in bfloat16 or wider, within the bound.
No kernel may reach another device: no remote copies, remote signals or barrier semaphores. Data moves between devices by JAX's collectives and lax.ppermute only.
A program may use at most 64 MiB of HBM per device.

v0:
```python
import jax
import jax.numpy as jnp
from jax import lax
from jax.sharding import PartitionSpec as P

TILE = 16


def with_halo(cells, sides, width):
    for axis, dim in sides:
        count = lax.axis_size(axis)
        ends = count - 1
        head = lax.slice_in_dim(cells, 0, width, axis=dim)
        tail = lax.slice_in_dim(cells, cells.shape[dim] - width, cells.shape[dim], axis=dim)
        cells = jnp.concatenate(
            [
                lax.ppermute(tail, axis, [(i, (i + 1) % count) for i in range(ends)]),
                cells,
                lax.ppermute(head, axis, [((i + 1) % count, i) for i in range(ends)]),
            ],
            axis=dim,
        )
    return cells


def banded(kernel, band_width):
    tap_count = kernel.shape[-1]
    span_len = band_width + tap_count - 1
    zero_tail = jnp.zeros(kernel.shape[:-1] + (band_width,), kernel.dtype)
    padded = jnp.concatenate([kernel, zero_tail], axis=-1)
    repeated = jnp.tile(padded, (1,) * (kernel.ndim - 1) + (band_width,))
    return repeated[..., : band_width * span_len].reshape(
        kernel.shape[:-1] + (band_width, span_len)
    )


def diagonals(matrix, tap_count):
    line_count = matrix.shape[-2]
    span_len = matrix.shape[-1]
    flattened = matrix.reshape(matrix.shape[:-2] + (line_count * span_len,))
    lead_len = (line_count - 1) * (span_len + 1)
    shaped = flattened[..., :lead_len].reshape(matrix.shape[:-2] + (line_count - 1, span_len + 1))
    last_line = flattened[..., lead_len : lead_len + tap_count]
    return jnp.sum(shaped[..., :tap_count], axis=-2) + last_line


def body(pattern, measured, row_kernels, col_kernels, tile_patch, sat_tiles):
    captures, colours, rows_ext, strip_width = pattern.shape
    height = measured.shape[2]
    tap_count = row_kernels.shape[-1]
    rim_width = (tap_count - 1) // 2
    tile_count = row_kernels.shape[0]
    patch_width = strip_width // tile_count
    extended = with_halo(pattern, (("field", 3),), rim_width)
    strip_tiles = strip_width // TILE
    across = strip_tiles * lax.axis_size("field")
    row_ids = jnp.arange(height // TILE, dtype=jnp.int32)
    col_ids = lax.axis_index("field") * strip_tiles + jnp.arange(strip_tiles, dtype=jnp.int32)
    tile_ids = row_ids[:, None] * across + col_ids[None, :]
    saturated = jnp.any(tile_ids[None, :, :, None] == sat_tiles[:, None, None, :], axis=-1)
    keep_tiles = 1.0 - saturated.astype(jnp.float32)
    keep_pixels = jnp.broadcast_to(
        keep_tiles[:, :, None, :, None], (captures, height // TILE, TILE, strip_tiles, TILE)
    ).reshape(captures, height, strip_width)
    slots = jnp.arange(tile_count, dtype=jnp.int32)
    selectors = []
    windows = []
    col_bands = []
    rowpasses = []
    partials = []
    for tile_index in range(tile_count):
        selector = (tile_patch[tile_index] == slots).astype(jnp.float32)
        row_taps = jnp.einsum("k,kqrb->qrb", selector, row_kernels.astype(jnp.float32)).astype(
            jnp.bfloat16
        )
        col_taps = jnp.einsum("k,kqrb->qrb", selector, col_kernels.astype(jnp.float32)).astype(
            jnp.bfloat16
        )
        row_band = banded(row_taps, patch_width)
        col_band = banded(col_taps, height)
        start = tile_index * patch_width
        window_cols = extended[..., start : start + patch_width + 2 * rim_width]
        rowpass = jnp.einsum(
            "cqyj,qrxj->cqryx", window_cols, row_band, preferred_element_type=jnp.float32
        ).astype(jnp.bfloat16)
        partial_tile = jnp.einsum(
            "qryk,cqrkx->cqyx", col_band, rowpass, preferred_element_type=jnp.float32
        )
        selectors.append(selector)
        windows.append(window_cols)
        col_bands.append(col_band)
        rowpasses.append(rowpass)
        partials.append(partial_tile)
    partial_value = jnp.concatenate(partials, axis=3)
    block_rows = height // lax.axis_size("bank")
    first_row = lax.axis_index("bank") * block_rows
    predicted_rows = lax.psum_scatter(partial_value, "bank", scatter_dimension=2, tiled=True)
    measured_rows = lax.dynamic_slice_in_dim(measured, first_row, block_rows, 2).astype(jnp.float32)
    keep_rows = lax.dynamic_slice_in_dim(keep_pixels, first_row, block_rows, 1)
    residual_rows = (keep_rows[:, None] * (predicted_rows - measured_rows)).astype(jnp.bfloat16)
    residual = lax.all_gather(residual_rows, "bank", axis=2, tiled=True)
    rank_count = row_kernels.shape[2]
    row_total = jnp.zeros((tile_count, colours, rank_count, tap_count), jnp.float32)
    col_total = jnp.zeros((tile_count, colours, rank_count, tap_count), jnp.float32)
    for tile_index in range(tile_count):
        start = tile_index * patch_width
        residual_tile = residual[..., start : start + patch_width]
        backward = jnp.einsum(
            "qryk,cqyx->cqrkx",
            col_bands[tile_index],
            residual_tile,
            preferred_element_type=jnp.float32,
        ).astype(jnp.bfloat16)
        row_terms = jnp.einsum(
            "cqrkx,cqkj->qrxj", backward, windows[tile_index], preferred_element_type=jnp.float32
        )
        col_terms = jnp.einsum(
            "cqyx,cqrkx->qryk",
            residual_tile,
            rowpasses[tile_index],
            preferred_element_type=jnp.float32,
        )
        row_grad = diagonals(row_terms, tap_count)
        col_grad = diagonals(col_terms, tap_count)
        row_total = row_total + selectors[tile_index][:, None, None, None] * row_grad[None]
        col_total = col_total + selectors[tile_index][:, None, None, None] * col_grad[None]
    summed_rows, summed_cols = lax.psum((row_total, col_total), "cap")
    return (summed_rows * (1.0 / height), summed_cols * (1.0 / height))


def solution(mesh):
    return jax.shard_map(
        body,
        mesh=mesh,
        in_specs=(
            P("cap", None, None, "field"),
            P("cap", None, None, "field"),
            P("field", None, "bank", None),
            P("field", None, "bank", None),
            P("field"),
            P("cap", None),
        ),
        out_specs=(P("field", None, "bank", None), P("field", None, "bank", None)),
        check_vma=False,
    )
```

profile of v0, /device:TPU:0, one launch (start us, length us, event | category | flops | bytes accessed | tf_op | source)
XLA Modules:
  0.0 204.7 jit_solution(9321753084598764518)
XLA Ops:
  7.3 3.0 %fusion.46 = (bf16[1,3,542,255]{3,2,1,0:T(8,128)(2,1)}, bf16[1,3,542,255]{3,2,1,0:T(8,128)(2,1)}) fusion(bf16[1,3,542,256]{3,2,1,0:T(8,128)(2,1)} %param.6), kind=kLoop, calls=%fused_computation.71 | loop fusion | bytes 3317040 | tf_op jit(solution)/shard_map/slice | solution.py:14
  10.2 5.8 %collective-permute-start = (bf16[1,3,542,255]{3,2,1,0:T(8,128)(2,1)}, bf16[1,3,542,255]{3,2,1,0:T(8,128)(2,1)}, u32[]{:S(2)}, u32[]{:S(2)}) collective-permute-start(bf16[1,3,542,255]{3,2,1,0:T(8,128)(2,1)} %get-tuple-element.4), channel_id=1, source_target_pairs={{0,16},{1,17},{2,18},{3,19},{4,20},{5,21},{6,22},{7,23},{8,24},{9,... | collective-permute-start | bytes 2487788 | tf_op jit(solution)/shard_map/ppermute | solution.py:17
  16.0 1.3 collective-permute-start.1
  17.3 0.6 fusion.47
  17.9 0.8 fusion.30
  18.7 0.8 fusion.34
  19.5 0.8 fusion.28
  20.3 0.8 fusion.32
  21.3 0.1 broadcast_add_fusion
  21.4 0.2 compare_reduce_fusion
  21.6 0.1 broadcast_in_dim.4
  21.7 0.1 broadcast_in_dim.5
  21.9 0.7 tile.43
  22.6 1.6 reshape.185
  24.2 0.7 tile.19
  25.0 1.6 reshape.181
  26.6 0.2 tile.40
  26.8 5.4 %tile.41 = bf16[3,4,81792]{2,1,0:T(4,128)(2,1)} reshape(bf16[3,4,128,639]{3,2,1,0:T(8,128)(2,1)S(1)} %tile.40) | data formatting | bytes 3926016 | tf_op jit(solution)/shard_map/tile | solution.py:31
  32.2 1.5 slice-done
  33.7 5.2 %reshape.182 = bf16[3,4,128,638]{3,2,1,0:T(8,128)(2,1)} reshape(bf16[3,4,81664]{2,1,0:T(4,128)(2,1)S(1)} %slice-done) | data formatting | bytes 3919872 | tf_op jit(solution)/shard_map/reshape | solution.py:32
  38.9 0.2 tile.16
  39.1 5.3 %tile.17 = bf16[3,4,81792]{2,1,0:T(4,128)(2,1)} reshape(bf16[3,4,128,639]{3,2,1,0:T(8,128)(2,1)S(1)} %tile.16) | data formatting | bytes 3926016 | tf_op jit(solution)/shard_map/tile | solution.py:31
  44.3 1.5 slice-done.1
  45.9 5.2 %reshape.178 = bf16[3,4,128,638]{3,2,1,0:T(8,128)(2,1)} reshape(bf16[3,4,81664]{2,1,0:T(4,128)(2,1)S(1)} %slice-done.1) | data formatting | bytes 3919872 | tf_op jit(solution)/shard_map/reshape | solution.py:32
  51.1 2.7 %pad_maximum_fusion = bf16[1,3,542,766]{3,2,1,0:T(8,128)(2,1)S(1)} fusion(bf16[1,3,542,255]{3,2,1,0:T(8,128)(2,1)} %collective-permute-done.1, bf16[1,3,542,256]{3,2,1,0:T(8,128)(2,1)S(1)} %copy-done.2, bf16[1,3,542,255]{3,2,1,0:T(8,128)(2,1)} %collective-permute-done), kind=kLoop, calls=%fused_computation.2 | loop fusion | flops 7473096 | bytes 4982064 | tf_op jit(solution)/shard_map/concatenate | solution.py:15
  53.9 1.5 fusion.4
  55.4 0.9 copy-done.7
  56.3 1.5 fusion.5
  57.8 0.4 fusion.25
  58.2 0.6 copy-done.10
  58.8 0.4 fusion.22
  59.3 0.6 pad_maximum_fusion.1
  59.9 0.0 all-reduce.7.cloned.1.call-start
  60.0 1.3 fusion.40
  61.3 21.4 %reduce-scatter.2.cloned.1.call-done = f32[1,3,8,256]{3,2,1,0:T(8,128)} async-done(((f32[1,3,32,256]{3,2,1,0:T(8,128)}), f32[1,3,8,256]{3,2,1,0:T(8,128)}) %reduce-scatter.2.cloned.1.call-update) | async-done | bytes 24592 | tf_op jit(solution)/shard_map/reduce_scatter | solution.py:97
  82.7 0.7 multiply_convert_fusion
  83.5 13.3 %all_gather.3 = bf16[1,3,32,256]{3,2,1,0:T(8,128)(2,1)S(1)} all-gather(bf16[1,3,8,256]{3,2,1,0:T(8,128)(2,1)S(1)} %multiply_convert_fusion), channel_id=1, replica_groups=mesh['field'=2,'cap'=4,'bank'=4] {'bank'}, dimensions={2}, use_global_device_ids=true | all-gather | bytes 61440 | tf_op jit(solution)/shard_map/all_gather | solution.py:101
  96.8 1.7 fusion.19
  98.4 1.7 fusion.16
  100.2 6.2 %fusion.2 = f32[3,4,128,638]{3,2,1,0:T(8,128)} fusion(bf16[1,3,542,766]{3,2,1,0:T(8,128)(2,1)} %copy-done.5, bf16[3,4,32,542]{3,2,1,0:T(8,128)(2,1)S(1)} %copy-done.9, bf16[1,3,32,256]{3,2,1,0:T(8,128)(2,1)S(1)} %all_gather.3), kind=kOutput, calls=%fused_computation.7 | convolution fusion | flops 1116398592 | bytes 6524928 | tf_op jit(solution)/shard_map/cqrkx,cqkj->qrxj/dot_general | solution.py:114
  106.4 6.3 %fusion = f32[3,4,128,638]{3,2,1,0:T(8,128)} fusion(bf16[1,3,542,766]{3,2,1,0:T(8,128)(2,1)} %copy-done.5, bf16[3,4,32,542]{3,2,1,0:T(8,128)(2,1)S(1)} %copy-done.11, bf16[1,3,32,256]{3,2,1,0:T(8,128)(2,1)S(1)} %all_gather.3), kind=kOutput, calls=%fused_computation.5 | convolution fusion | flops 1116398592 | bytes 6524928 | tf_op jit(solution)/shard_map/cqrkx,cqkj->qrxj/dot_general | solution.py:114
  112.6 1.0 reshape.194
  113.6 0.2 copy-done.3
  113.8 1.0 reshape.196
  114.8 0.1 slice.113
  114.9 2.0 reshape.197
  116.9 1.3 slice_reduce_fusion.2
  118.1 0.1 slice.110
  118.2 2.0 reshape.195
  120.2 1.3 slice_reduce_fusion.3
  121.4 7.2 %reshape.192 = f32[3,4,81664]{2,1,0:T(4,128)} reshape(f32[3,4,128,638]{3,2,1,0:T(8,128)} %fusion.2) | data formatting | bytes 7839744 | tf_op jit(solution)/shard_map/reshape | solution.py:40
  128.6 6.9 %reshape.188 = f32[3,4,81664]{2,1,0:T(4,128)} reshape(f32[3,4,128,638]{3,2,1,0:T(8,128)} %fusion) | data formatting | bytes 7839744 | tf_op jit(solution)/shard_map/reshape | solution.py:40
  135.6 4.3 %slice.103 = f32[3,4,81153]{2,1,0:T(4,128)} slice(f32[3,4,81664]{2,1,0:T(4,128)} %reshape.188), slice={[0:3], [0:4], [0:81153]} | slice | bytes 7790688 | tf_op jit(solution)/shard_map/slice | solution.py:42
  139.8 7.3 %reshape.189 = f32[3,4,127,639]{3,2,1,0:T(8,128)} reshape(f32[3,4,81153]{2,1,0:T(4,128)} %slice.103) | data formatting | bytes 7790688 | tf_op jit(solution)/shard_map/reshape | solution.py:42
  147.1 2.3 %slice_reduce_fusion.1 = f32[3,4,511]{2,1,0:T(4,128)S(1)} fusion(f32[3,4,127,639]{3,2,1,0:T(8,128)} %reshape.189), kind=kLoop, calls=%fused_computation.1 | loop fusion | flops 772632 | bytes 3139584 | tf_op jit(solution)/shard_map/reduce_sum | solution.py:44
  149.4 4.3 %slice.107 = f32[3,4,81153]{2,1,0:T(4,128)} slice(f32[3,4,81664]{2,1,0:T(4,128)} %reshape.192), slice={[0:3], [0:4], [0:81153]} | slice | bytes 7790688 | tf_op jit(solution)/shard_map/slice | solution.py:42
  153.7 7.3 %reshape.193 = f32[3,4,127,639]{3,2,1,0:T(8,128)} reshape(f32[3,4,81153]{2,1,0:T(4,128)} %slice.107) | data formatting | bytes 7790688 | tf_op jit(solution)/shard_map/reshape | solution.py:42
  161.0 2.3 %slice_reduce_fusion = f32[3,4,511]{2,1,0:T(4,128)S(1)} fusion(f32[3,4,127,639]{3,2,1,0:T(8,128)} %reshape.193), kind=kLoop, calls=%fused_computation | loop fusion | flops 772632 | bytes 3139584 | tf_op jit(solution)/shard_map/reduce_sum | solution.py:44
  163.3 0.1 slice_add_fusion
  163.3 0.8 slice_add_fusion.2
  164.2 0.7 multiply_add_fusion
  165.0 30.0 %all-reduce.7.cloned.1.call-done = (f32[2,3,4,511]{3,2,1,0:T(4,128)}, f32[2,3,4,511]{3,2,1,0:T(4,128)}) async-done(((f32[2,3,4,511]{3,2,1,0:T(4,128)}, f32[2,3,4,511]{3,2,1,0:T(4,128)}), (f32[2,3,4,511]{3,2,1,0:T(4,128)}, f32[2,3,4,511]{3,2,1,0:T(4,128)})) %all-reduce.7.cloned.1.call-update) | async-done | bytes 98128 | tf_op jit(solution)/shard_map/psum | solution.py:127
  195.0 1.4 broadcast_multiply_fusion.1
  196.4 1.4 broadcast_multiply_fusion
  (48 shorter events, 0.3 us)
Async XLA Ops:
  7.2 10.7 %copy-start = (bf16[2,3,4,511]{3,2,1,0:T(4,128)(2,1)S(1)}, bf16[2,3,4,511]{3,2,1,0:T(4,128)(2,1)}, u32[]{:S(2)}) copy-start(bf16[2,3,4,511]{3,2,1,0:T(4,128)(2,1)} %param.9) | copy-start | bytes 73588
  7.2 10.1 %copy-start.12 = (s32[2]{0:T(128)S(1)}, s32[2]{0:T(128)}, u32[]{:S(2)}) copy-start(s32[2]{0:T(128)} %param.10) | copy-start | bytes 28
  7.2 11.5 %copy-start.14 = (bf16[2,3,4,511]{3,2,1,0:T(4,128)(2,1)S(1)}, bf16[2,3,4,511]{3,2,1,0:T(4,128)(2,1)}, u32[]{:S(2)}) copy-start(bf16[2,3,4,511]{3,2,1,0:T(4,128)(2,1)} %param.8) | copy-start | bytes 73588
  7.2 14.2 %copy-start.13 = (s32[1,256]{1,0:T(1,128)S(1)}, s32[1,256]{1,0:T(1,128)}, u32[]{:S(2)}) copy-start(s32[1,256]{1,0:T(1,128)} %param.11) | copy-start | bytes 3076
  7.2 75.5 %reduce-scatter.2.cloned.1.call-start = ((), (), s32[]{:S(2)}) async-start(), calls=%async_computation.1 | async-start | bytes 122880 | tf_op jit(solution)/shard_map/reduce_scatter | solution.py:97
  10.2 40.9 %collective-permute-start = (bf16[1,3,542,255]{3,2,1,0:T(8,128)(2,1)}, bf16[1,3,542,255]{3,2,1,0:T(8,128)(2,1)}, u32[]{:S(2)}, u32[]{:S(2)}) collective-permute-start(bf16[1,3,542,255]{3,2,1,0:T(8,128)(2,1)} %get-tuple-element.4), channel_id=1, source_target_pairs={{0,16},{1,17},{2,18},{3,19},{4,20},{5,21},{6,22},{7,23},{8,24},{9,... | collective-permute-start | bytes 2487788 | tf_op jit(solution)/shard_map/ppermute | solution.py:17
  16.0 35.1 %collective-permute-start.1 = (bf16[1,3,542,255]{3,2,1,0:T(8,128)(2,1)}, bf16[1,3,542,255]{3,2,1,0:T(8,128)(2,1)}, u32[]{:S(2)}, u32[]{:S(2)}) collective-permute-start(bf16[1,3,542,255]{3,2,1,0:T(8,128)(2,1)} %get-tuple-element.5), channel_id=1, source_target_pairs={{16,0},{17,1},{18,2},{19,3},{20,4},{21,5},{22,6},{23,7},{24,8},{25... | collective-permute-start | bytes 2487788 | tf_op jit(solution)/shard_map/ppermute | solution.py:19
  32.2 1.5 slice-start
  44.3 1.5 slice-start.1
  45.9 5.3 %copy-start.2 = (bf16[1,3,542,256]{3,2,1,0:T(8,128)(2,1)S(1)}, bf16[1,3,542,256]{3,2,1,0:T(8,128)(2,1)}, u32[]{:S(2)}) copy-start(bf16[1,3,542,256]{3,2,1,0:T(8,128)(2,1)} %param.6) | copy-start | bytes 2497540
  51.1 2.7 %copy-start.6 = (bf16[3,4,128,638]{3,2,1,0:T(8,128)(2,1)S(1)}, bf16[3,4,128,638]{3,2,1,0:T(8,128)(2,1)}, u32[]{:S(2)}) copy-start(bf16[3,4,128,638]{3,2,1,0:T(8,128)(2,1)} %reshape.182) | copy-start | bytes 5879812
  53.8 1.5 copy-start.5
  53.9 2.5 %copy-start.7 = (bf16[3,4,128,638]{3,2,1,0:T(8,128)(2,1)S(1)}, bf16[3,4,128,638]{3,2,1,0:T(8,128)(2,1)}, u32[]{:S(2)}) copy-start(bf16[3,4,128,638]{3,2,1,0:T(8,128)(2,1)} %reshape.178) | copy-start | bytes 5879812
  56.3 1.5 copy-start.8
  57.8 1.0 copy-start.10
  59.9 135.1 %all-reduce.7.cloned.1.call-start = ((), (), s32[]{:S(2)}) async-start(), calls=%async_computation.2 | async-start | bytes 196608 | tf_op jit(solution)/shard_map/psum | solution.py:127
  98.4 1.7 copy-start.9
  100.2 6.2 %copy-start.11 = (bf16[3,4,32,542]{3,2,1,0:T(8,128)(2,1)S(1)}, bf16[3,4,32,542]{3,2,1,0:T(8,128)(2,1)}, u32[]{:S(2)}) copy-start(bf16[3,4,32,542]{3,2,1,0:T(8,128)(2,1)} %reshape.181) | copy-start | bytes 1248772
  106.4 6.3 %copy-start.4 = (f32[3,4,32,542]{3,2,1,0:T(8,128)S(1)}, f32[3,4,32,542]{3,2,1,0:T(8,128)}, u32[]{:S(2)}) copy-start(f32[3,4,32,542]{3,2,1,0:T(8,128)} %fusion.16) | copy-start | bytes 2497540
  112.6 1.2 copy-start.3
  153.7 44.2 %copy-start.1 = (bf16[2,3,4,511]{3,2,1,0:T(4,128)(2,1)S(1)}, bf16[2,3,4,511]{3,2,1,0:T(4,128)(2,1)}, u32[]{:S(2)}) copy-start(bf16[2,3,4,511]{3,2,1,0:T(4,128)(2,1)} %param.9) | copy-start | bytes 73588
Sparse Core Ops, SparseCore 0:
  60.0 22.6 reduce-scatter.1
  165.1 29.8 all-reduce.6
where the time goes:
time: 206 us; the launch traced here: 205 us
  local copies, waits for them, and re-layouts  78.3 us (38%)
  waiting for transfers between devices  51.5 us (25%)
  matrix products  22.8 us (11%)
  other arithmetic  17.2 us (8%)
  between operations  14.4 us (7%)
  blocking collectives  13.3 us (6%)
  starting transfers between devices  7.13 us (3%)
    psum x1, waiting for transfers between devices, body(): summed_rows, summed_cols = lax.psum((row_total, col_total), 'cap')  30 us
    reduce_scatter x1, waiting for transfers between devices, body(): lax.psum_scatter(partial_value, 'bank', scatter_dimension=2, tiled=True)  21.4 us
    reshape x4, local copies, waits for them, and re-layouts, diagonals(): flattened[..., :lead_len]  18.6 us
    reshape x4, local copies, waits for them, and re-layouts, diagonals(): flattened = matrix.reshape(matrix.shape[:-2] + (line_count * span_len,))  16.1 us
    reshape x4, local copies, waits for them, and re-layouts, banded(): repeated[..., :band_width * span_len]  13.7 us
    all_gather x1, blocking collectives, body(): residual = lax.all_gather(residual_rows, 'bank', axis=2, tiled=True)  13.3 us
    another operation x8, local copies, waits for them, and re-layouts, banded(): repeated = jnp.tile(padded, (1,) * (kernel.ndim - 1) + (band_width,))  12.5 us
    dot_general x2, matrix products, body(): jnp.einsum('cqrkx,cqkj->qrxj', backward, windows[tile_index], preferred_e...  12.5 us
  transfers between devices with their start and end apart: 4, of which 2 were waited for; matrix products, arithmetic and copies ran while one was open for 16% of the time, Pallas kernels for 0%

commit v1 on v0

v1 whole, which is shorter than its diff:
```python
import functools

import jax
import jax.numpy as jnp
from jax import lax
from jax.experimental import pallas as pl
from jax.experimental.pallas import tpu as pltpu
from jax.sharding import PartitionSpec as P

TILE = 16
BF = jnp.bfloat16
F32 = jnp.float32
NT = (((1,), (1,)), ((), ()))
NN = (((1,), (0,)), ((), ()))
TN = (((0,), (0,)), ((), ()))


def dot(a, b, dims):
    return lax.dot_general(a, b, dims, preferred_element_type=F32)


def exchange(cells, axis, step):
    count = lax.axis_size(axis)
    return lax.ppermute(cells, axis, [(i, i ^ step) for i in range(count)])


def pad_rows(dst, lanes, rows_ref, rows):
    width = rows_ref.shape[-1]
    depth = dst.shape[0]
    whole = rows // 16 * 16
    dst[whole:depth, lanes : lanes + width] = jnp.zeros((depth - whole, width), BF)
    dst[0:rows, lanes : lanes + width] = rows_ref[...]


def triangle(side, patch, width, strip):
    x = lax.broadcasted_iota(jnp.int32, (width, strip), 0) + patch * width
    j = lax.broadcasted_iota(jnp.int32, (width, strip), 1)
    left = (j > x).astype(jnp.int32)
    right = (j < x).astype(jnp.int32)
    return (side * left + (1 - side) * right) > 0


def front(
    dims, scalars, w_ref, *refs
):
    pieces, n_nb, tiles, width, strip, rows, height = dims
    kern = refs[: len(pieces)]
    band_nb, band_own, cols_out, v_own, pred, wp, band_all, vl = refs[len(pieces) :]
    lanes = 2 * strip
    depth = wp.shape[0]
    pad_rows(wp, 0, w_ref.at[0, 0], rows)
    for t in range(tiles):
        pick = scalars[t]
        masks = [triangle(scalars[tiles + n], t, width, strip) for n in range(n_nb)]
        slot = 0
        for piece, slots in zip(kern, pieces):
            for s in range(slots):
                row_taps = piece[s, 0, pick, 0].astype(F32)
                col_taps = piece[s, 1, pick, 0].astype(F32)
                ranks = row_taps.shape[0]
                col_taps = jnp.concatenate(
                    [col_taps, jnp.zeros((ranks, depth - col_taps.shape[1]), F32)], axis=1
                )
                for r in range(ranks):
                    at = slot * strip
                    one = jnp.broadcast_to(row_taps[r : r + 1], (16, lanes))
                    base = pltpu.roll(one, 1 + t * width, 1, stride=1, stride_axis=0).astype(BF)
                    for g in range(width // 16):
                        tile = base if g == 0 else pltpu.roll(base, 16 * g, 1)
                        span = slice(16 * g, 16 * g + 16)
                        for n in range(n_nb):
                            kept = jnp.where(masks[n][span], tile[:, :strip].astype(F32), 0.0)
                            band_nb[0, n, t, span, at : at + strip] = kept.astype(BF)
                        band_all[span, at : at + strip] = tile[:, strip:]
                    one = jnp.broadcast_to(col_taps[r : r + 1], (height, depth))
                    cols = pltpu.roll(one, 0, 1, stride=1, stride_axis=0).astype(BF)
                    cols_out[0, t, slot * height : (slot + 1) * height, :] = cols
                    slot += 1
        keep = band_own.shape[-1]
        band_own[0, t] = band_all[:, :keep]
        v = dot(cols_out[0, t], wp[...], NN).astype(BF)
        for r in range(slot):
            vl[:, r * strip : (r + 1) * strip] = v[r * height : (r + 1) * height]
        v_own[0, t] = vl[:, :keep]
        pred[0, t * width : (t + 1) * width, :] = dot(band_all[...], vl[...], NT)


def fold(rows, shift_groups):
    total = rows[0:8]
    for g in range(1, rows.shape[0] // 8):
        total = total + pltpu.roll(rows[8 * g : 8 * g + 8], rows.shape[1] - 8 * g, 1)
    return total


def settle(acc):
    count, lanes = acc.shape
    sub = lax.broadcasted_iota(jnp.int32, acc.shape, 0)
    for bit in (1, 2, 4):
        acc = jnp.where((sub & bit) != 0, pltpu.roll(acc, lanes - bit, 1), acc)
    return jnp.sum(acc.reshape(count // 8, 8, lanes), axis=1)


def back(dims, scalars, w_own, *refs):
    n_nb, tiles, width, strip, rows, height, ranks, scale = dims
    halos = refs[:n_nb]
    (band_nb, band_own, cols, v_own, pred, base, keep, out, wp, vl, vn, us, acc) = refs[n_nb:]
    all_ranks = cols.shape[2] // height
    lanes = 2 * strip
    for n in range(n_nb):
        pad_rows(wp, n * strip, halos[n].at[0, 0], rows)
    pad_rows(wp, n_nb * strip, w_own.at[0, 0], rows)
    for t in range(tiles):
        span = slice(t * width, (t + 1) * width)
        total = pred[0, span, :]
        for n in range(n_nb):
            v = dot(cols[0, t], wp[:, n * strip : (n + 1) * strip], NN).astype(BF)
            for r in range(all_ranks):
                vl[:, r * strip : (r + 1) * strip] = v[r * height : (r + 1) * height]
            vn[n] = vl[:, : ranks * strip]
            total = total + dot(band_nb[0, n, t], vl[...], NT)
        res_t = (keep[span, :] * (total - base[0, span, :])).astype(BF)
        for r in range(ranks):
            at = slice(r * strip, (r + 1) * strip)
            near = dot(res_t, v_own[0, t, :, at], NN)
            far = jnp.zeros((width, strip), F32)
            for n in range(n_nb):
                mask = triangle(scalars[tiles + n], t, width, strip)
                far = far + jnp.where(mask, dot(res_t, vn[n, :, at], NN), 0.0)
            both = jnp.concatenate([far, near], axis=1)
            part = fold(both, 0)
            acc[8 * (t * ranks + r) : 8 * (t * ranks + r) + 8, :lanes] = pltpu.roll(
                part, lanes - (t * width + 1), 1
            )
        for n in range(n_nb + 1):
            bands = band_own[0, t] if n == n_nb else band_nb[0, n, t, :, : ranks * strip]
            u = dot(res_t, bands, TN).astype(BF)
            for r in range(ranks):
                first = (t * ranks + r) * height
                us[first : first + height, n * strip : (n + 1) * strip] = u[
                    :, r * strip : (r + 1) * strip
                ]
    row_grads = settle(acc[...]) * scale
    z = dot(us[...], wp[...], NT)
    for i in range(tiles * ranks):
        acc_z = fold(z[i * height : (i + 1) * height], 0)
        wp_z = settle(acc_z)
        col = wp_z[:, :lanes] * scale
        row = row_grads[i : i + 1]
        t, r = divmod(i, ranks)
        for s in range(tiles):
            hit = (scalars[t] == s).astype(F32)
            if t == 0:
                out[0, 0, s, r : r + 1, :] = hit * row
                out[0, 1, s, r : r + 1, :] = hit * col
            else:
                out[0, 0, s, r : r + 1, :] += hit * row
                out[0, 1, s, r : r + 1, :] += hit * col


def body(pattern, measured, row_kernels, col_kernels, tile_patch, sat_tiles):
    _, colours, rows, strip = pattern.shape
    height = measured.shape[2]
    tiles, _, ranks, taps = row_kernels.shape
    width = strip // tiles
    lanes = 2 * strip
    depth = -(-rows // 128) * 128
    fields = lax.axis_size("field")
    banks = lax.axis_size("bank")
    caps = lax.axis_size("cap")
    here = lax.axis_index("field")

    if fields == 2:
        halos = [exchange(pattern, "field", 1)]
        sides = [here]
    else:
        halos = [
            lax.ppermute(pattern, "field", [(i, i + 1) for i in range(fields - 1)]),
            lax.ppermute(pattern, "field", [(i + 1, i) for i in range(fields - 1)]),
        ]
        sides = [jnp.ones_like(here), jnp.zeros_like(here)]
    n_nb = len(halos)

    kern = jnp.stack([row_kernels, col_kernels])
    kern = jnp.pad(kern, ((0, 0),) * 4 + ((0, lanes - taps),))[None]
    pieces = [kern]
    step = 1
    while step < banks:
        held = pieces[0] if len(pieces) == 1 else jnp.concatenate(pieces, axis=0)
        pieces.append(exchange(held, "bank", step))
        step *= 2
    counts = tuple(p.shape[0] for p in pieces)
    all_ranks = sum(counts) * ranks

    scalars = jnp.concatenate([tile_patch, jnp.stack(sides).astype(jnp.int32)])

    strip_tiles = strip // TILE
    across = strip_tiles * fields
    row_ids = jnp.arange(height // TILE, dtype=jnp.int32)
    col_ids = here * strip_tiles + jnp.arange(strip_tiles, dtype=jnp.int32)
    tile_ids = col_ids[:, None] + row_ids[None, :] * across
    saturated = jnp.any(tile_ids[:, :, None] == sat_tiles[0][None, None, :], axis=-1)
    keep = 1.0 - saturated.astype(F32)
    keep = jnp.broadcast_to(
        keep[:, None, :, None], (strip_tiles, TILE, height // TILE, TILE)
    ).reshape(strip, height)
    base = jnp.swapaxes(measured[0], 1, 2).astype(F32)

    vmem = pltpu.VMEM
    params = pltpu.CompilerParams(
        dimension_semantics=("arbitrary",), vmem_limit_bytes=40 * 2**20
    )

    def per_colour(shape):
        nd = len(shape)
        return pl.BlockSpec((1,) + shape, lambda q, *_: (q,) + (0,) * nd)

    smem = pl.BlockSpec(memory_space=pltpu.SMEM)
    w_spec = pl.BlockSpec((1, 1, rows, strip), lambda q: (0, q, 0, 0))
    band_nb_s = (n_nb, tiles, width, all_ranks * strip)
    band_own_s = (tiles, width, ranks * strip)
    cols_s = (tiles, all_ranks * height, depth)
    v_own_s = (tiles, height, ranks * strip)
    pred_s = (strip, height)
    shapes = [
        (band_nb_s, BF),
        (band_own_s, BF),
        (cols_s, BF),
        (v_own_s, BF),
        (pred_s, F32),
    ]
    fronts = pl.pallas_call(
        functools.partial(front, (counts, n_nb, tiles, width, strip, rows, height)),
        grid=(colours,),
        in_specs=[smem, w_spec]
        + [
            pl.BlockSpec((c, 2, tiles, 1, ranks, lanes), lambda q: (0, 0, 0, q, 0, 0))
            for c in counts
        ],
        out_specs=[per_colour(s) for s, _ in shapes],
        out_shape=[jax.ShapeDtypeStruct((colours,) + s, d) for s, d in shapes],
        scratch_shapes=[
            vmem((depth, strip), BF),
            vmem((width, all_ranks * strip), BF),
            vmem((height, all_ranks * strip), BF),
        ],
        compiler_params=params,
        name="front",
    )(scalars, pattern, *pieces)

    out_s = (2, tiles, ranks, lanes)
    grads = pl.pallas_call(
        functools.partial(
            back, (n_nb, tiles, width, strip, rows, height, ranks, 1.0 / height)
        ),
        grid=(colours,),
        in_specs=[smem, w_spec]
        + [w_spec] * n_nb
        + [per_colour(s) for s, _ in shapes]
        + [per_colour(pred_s), pl.BlockSpec((strip, height), lambda q: (0, 0))],
        out_specs=per_colour(out_s),
        out_shape=jax.ShapeDtypeStruct((colours,) + out_s, F32),
        scratch_shapes=[
            vmem((depth, (n_nb + 1) * strip), BF),
            vmem((height, all_ranks * strip), BF),
            vmem((n_nb, height, ranks * strip), BF),
            vmem((tiles * ranks * height, (n_nb + 1) * strip), BF),
            vmem((8 * tiles * ranks, lanes), F32),
        ],
        compiler_params=params,
        name="back",
    )(scalars, pattern, *halos, *fronts, base, keep)

    step = caps // 2
    while step:
        grads = grads + exchange(grads, "cap", step)
        step //= 2
    grads = jnp.moveaxis(grads, 0, 2)[..., :taps]
    return grads[0], grads[1]


def solution(mesh):
    return jax.shard_map(
        body,
        mesh=mesh,
        in_specs=(
            P("cap", None, None, "field"),
            P("cap", None, None, "field"),
            P("field", None, "bank", None),
            P("field", None, "bank", None),
            P("field"),
            P("cap", None),
        ),
        out_specs=(P("field", None, "bank", None), P("field", None, "bank", None)),
        check_vma=False,
    )
```

time: 206 us -> 47.6 us (0.23)
  local copies, waits for them, and re-layouts: 78.3 us -> 6.35 us
  waiting for transfers between devices: 51.5 us -> 8.06 us
  matrix products: 22.8 us -> 0 us
  Pallas kernels: 0 us -> 20.5 us
  other arithmetic: 17.2 us -> 2.62 us
  between operations: 14.4 us -> 0.72 us
  blocking collectives: 13.3 us -> 0 us
    reshape x12 -> x2, local copies, waits for them, and re-layouts: 48.3 us -> 0.25 us  [body(): keep = jnp.broadcast_to(keep[:, None, :, None], (strip_tiles, TILE, heigh...]
    psum x1 -> x0, waiting for transfers between devices: 30 us -> none  [body(): summed_rows, summed_cols = lax.psum((row_total, col_total), 'cap')]
    dot_general x12 -> x0, matrix products: 22.8 us -> none  [the longest x2 12.5 us: body(): jnp.einsum('cqrkx,cqkj->qrxj', backward, windows[tile_index], preferred_e...]
    reduce_scatter x1 -> x0, waiting for transfers between devices: 21.4 us -> none  [body(): lax.psum_scatter(partial_value, 'bank', scatter_dimension=2, tiled=True)]
    pallas_call x0 -> x2, Pallas kernels: none -> 20.5 us  [the longest x1 11.7 us: body(): pl.pallas_call(functools.partial(back, (n_nb, tiles, width, strip, rows,...]
    slice x10 -> x0, local copies, waits for them, and re-layouts: 15.3 us -> none  [the longest x4 8.67 us: diagonals(): flattened[..., :lead_len]]
    all_gather x1 -> x0, blocking collectives: 13.3 us -> none  [body(): residual = lax.all_gather(residual_rows, 'bank', axis=2, tiled=True)]
    another operation x9 -> x0, local copies, waits for them, and re-layouts: 12.5 us -> none  [the longest x8 12.5 us: banded(): repeated = jnp.tile(padded, (1,) * (kernel.ndim - 1) + (band_width,))]
  transfers between devices with their start and end apart: 4 -> 5, of which waited for: 2 -> 4; matrix products, arithmetic and copies ran while one was open for 16% -> 8% of each run, Pallas kernels for 0% -> 19%
where the time goes in v1:
time: 47.6 us; the launch traced here: 47.3 us
  Pallas kernels  20.5 us (43%)
  starting transfers between devices  8.98 us (19%)
  waiting for transfers between devices  8.06 us (17%)
  local copies, waits for them, and re-layouts  6.35 us (13%)
  other arithmetic  2.62 us (6%)
  between operations  0.72 us (2%)
    pallas_call x1, Pallas kernels, body(): pl.pallas_call(functools.partial(back, (n_nb, tiles, width, strip, rows,...  11.7 us
    ppermute x5, starting transfers between devices, exchange(): return lax.ppermute(cells, axis, [(i, i ^ step) for i in range(count)])  8.98 us
    pallas_call x1, Pallas kernels, body(): pl.pallas_call(functools.partial(front, (counts, n_nb, tiles, width, stri...  8.85 us
    ppermute x5, waiting for transfers between devices, exchange(): return lax.ppermute(cells, axis, [(i, i ^ step) for i in range(count)])  8.06 us
    unnamed x7, local copies, waits for them, and re-layouts  6.01 us
  transfers between devices with their start and end apart: 5, of which 4 were waited for; matrix products, arithmetic and copies ran while one was open for 8% of the time, Pallas kernels for 19%

profile of v1, /device:TPU:0, one launch (start us, length us, event | category | flops | bytes accessed | tf_op | source)
XLA Modules:
  0.0 47.3 jit_solution(2161947339301512947)
XLA Ops:
  0.6 3.0 %collective-permute-start = (bf16[1,3,542,256]{3,2,1,0:T(8,128)(2,1)}, bf16[1,3,542,256]{3,2,1,0:T(8,128)(2,1)S(1)}, u32[]{:S(2)}, u32[]{:S(2)}) collective-permute-start(bf16[1,3,542,256]{3,2,1,0:T(8,128)(2,1)} %w_own.1), channel_id=1, source_target_pairs={{0,16},{16,0},{1,17},{17,1},{2,18},{18,2},{3,19},{19,3},{4,20},{20... | collective-permute-start | bytes 2497544 | tf_op jit(solution)/shard_map/ppermute | solution.py:24
  3.7 0.8 %fusion.3.refs_0_ = bf16[1,2,2,3,4,512]{5,4,3,2,1,0:T(4,128)(2,1)S(1)} fusion(bf16[1,2,3,4,511]{4,3,2,1,0:T(4,128)(2,1)} %bitcast.21, bf16[1,2,3,4,511]{4,3,2,1,0:T(4,128)(2,1)} %bitcast.22), kind=kLoop, calls=%fused_computation.7 | loop fusion | flops 172032 | bytes 98208 | tf_op jit(solution)/shard_map/broadcast_in_dim | solution.py:184
  4.4 1.6 %collective-permute-start.1 = (bf16[1,2,2,3,4,512]{5,4,3,2,1,0:T(4,128)(2,1)S(1)}, bf16[1,2,2,3,4,512]{5,4,3,2,1,0:T(4,128)(2,1)S(1)}, u32[]{:S(2)}, u32[]{:S(2)}) collective-permute-start(bf16[1,2,2,3,4,512]{5,4,3,2,1,0:T(4,128)(2,1)S(1)} %fusion.3.refs_0_), channel_id=1, source_target_pairs={{0,1},{1,0},{2,3},{3,2},{4,5},{5,4},{6,7},{7,6},{8,9},{9,8},{10,11... | collective-permute-start | bytes 147464 | tf_op jit(solution)/shard_map/ppermute | solution.py:24
  6.1 0.1 broadcast_add_fusion
  6.2 1.0 %copy.15 = bf16[1,3,32,256]{2,3,1,0:T(8,128)(2,1)S(1)} copy(bf16[1,3,32,256]{3,2,1,0:T(8,128)(2,1)} %param.7) | data formatting | bytes 98304 | tf_op args[1]
  7.1 0.9 %compare_reduce_fusion = pred[16,2]{0,1:T(4,128)(4,1)S(1)} fusion(s32[256]{0:T(256)} %bitcast.23, s32[16,2]{0,1:T(2,128)S(1)} %broadcast_add_fusion), kind=kLoop, calls=%fused_computation.10 | loop fusion | flops 16352 | bytes 1184 | tf_op jit(solution)/shard_map/reduce_or | solution.py:201
  8.1 0.1 broadcast_in_dim.5
  8.1 0.1 reshape.50
  8.3 0.1 copy.16.refs_7_
  8.4 0.2 collective-permute-done.1.refs_1_
  8.6 0.1 pad_maximum_fusion
  8.7 2.7 %collective-permute-start.2 = (bf16[2,2,2,3,4,512]{5,4,3,2,1,0:T(4,128)(2,1)S(1)}, bf16[2,2,2,3,4,512]{5,4,3,2,1,0:T(4,128)(2,1)S(1)}, u32[]{:S(2)}, u32[]{:S(2)}) collective-permute-start(bf16[2,2,2,3,4,512]{5,4,3,2,1,0:T(4,128)(2,1)S(1)} %pad_maximum_fusion), channel_id=1, source_target_pairs={{0,2},{1,3},{2,0},{3,1},{4,6},{5,7},{6,4},{7,5},{8,10},{9,11},{10,... | collective-permute-start | bytes 294920 | tf_op jit(solution)/shard_map/ppermute | solution.py:24
  11.3 0.7 %pad_add_fusion.scalars = s32[3]{0:T(128)S(1)} fusion(s32[1]{0:T(128)} %bitcast, s32[2]{0:T(128)} %param.10), kind=kLoop, calls=%fused_computation.12 | loop fusion | flops 3 | bytes 24 | tf_op jit(solution)/shard_map/concatenate | solution.py:194
  12.1 3.5 %collective-permute-done.2.refs_2_ = bf16[2,2,2,3,4,512]{5,4,3,2,1,0:T(4,128)(2,1)S(1)} collective-permute-done((bf16[2,2,2,3,4,512]{5,4,3,2,1,0:T(4,128)(2,1)S(1)}, bf16[2,2,2,3,4,512]{5,4,3,2,1,0:T(4,128)(2,1)S(1)}, u32[]{:S(2)}, u32[]{:S(2)}) %collective-permute-start.2) | collective-permute-done | bytes 98336 | tf_op jit(solution)/shard_map/ppermute | solution.py:24
  15.5 0.0 copy-start.1
  15.5 1.1 %copy-done.1 = bf16[1,3,542,256]{3,2,1,0:T(8,128)(2,1)S(1)} copy-done((bf16[1,3,542,256]{3,2,1,0:T(8,128)(2,1)S(1)}, bf16[1,3,542,256]{3,2,1,0:T(8,128)(2,1)}, u32[]{:S(2)}) %copy-start.1) | copy-done | bytes 832536
  16.7 8.8 %front.1 = (bf16[3,1,2,128,4096]{4,3,2,1,0:T(8,128)(2,1)S(1)}, bf16[3,2,128,1024]{3,2,1,0:T(8,128)(2,1)S(1)}, bf16[3,2,512,640]{3,2,1,0:T(8,128)(2,1)S(1)}, bf16...) custom-call(s32[3]{0:T(128)S(1)} %pad_add_fusion.scalars, bf16[1,3,542,256]{3,2,1,0:T(8,128)(2,1)S(1)} %copy-done.1, ...), custom_call_target="tpu_custom_call" | custom-call | tf_op jit(solution)/shard_map/front/pallas_call | solution.py:231
  25.5 0.0 copy-start
  25.5 2.7 %copy-done = bf16[3,1,2,128,4096]{4,3,2,1,0:T(8,128)(2,1)} copy-done((bf16[3,1,2,128,4096]{4,3,2,1,0:T(8,128)(2,1)}, bf16[3,1,2,128,4096]{4,3,2,1,0:T(8,128)(2,1)S(1)}, u32[]{:S(2)}) %copy-start) | copy-done | bytes 6291480
  28.2 0.0 collective-permute-done.refs_0_
  28.2 11.7 %back.1 = f32[3,2,2,4,512]{4,3,2,1,0:T(4,128)S(1)} custom-call(s32[3]{0:T(128)S(1)} %pad_add_fusion.scalars, bf16[1,3,542,256]{3,2,1,0:T(8,128)(2,1)S(1)} %copy-done.1, bf16[1,3,542,256]{3,2,1,0:T(8,128)(2,1)S(1)} %collective-permute-done.refs_0_, bf16[3,1,2,128,4096]{4,3,2,1,0:T(8,128)(2,1)} %copy-done, ...), custom_call_target="tpu_custom_call" | custom-call | tf_op jit(solution)/shard_map/back/pallas_call | solution.py:251
  39.9 1.6 %collective-permute-start.3 = (f32[3,2,2,4,512]{4,3,2,1,0:T(4,128)S(1)}, f32[3,2,2,4,512]{4,3,2,1,0:T(4,128)S(1)}, u32[]{:S(2)}, u32[]{:S(2)}) collective-permute-start(f32[3,2,2,4,512]{4,3,2,1,0:T(4,128)S(1)} %back.1), channel_id=1, source_target_pairs={{0,8},{4,12},{8,0},{12,4},{1,9},{5,13},{9,1},{13,5},{2,10},{6,14},... | collective-permute-start | bytes 294920 | tf_op jit(solution)/shard_map/ppermute | solution.py:24
  41.5 3.1 %collective-permute-done.3 = f32[3,2,2,4,512]{4,3,2,1,0:T(4,128)S(1)} collective-permute-done((f32[3,2,2,4,512]{4,3,2,1,0:T(4,128)S(1)}, f32[3,2,2,4,512]{4,3,2,1,0:T(4,128)S(1)}, u32[]{:S(2)}, u32[]{:S(2)}) %collective-permute-start.3) | collective-permute-done | bytes 98336 | tf_op jit(solution)/shard_map/ppermute | solution.py:24
  44.6 0.1 collective-permute-start.4
  44.7 1.3 %collective-permute-done.4 = f32[3,2,2,4,512]{4,3,2,1,0:T(4,128)S(1)} collective-permute-done((f32[3,2,2,4,512]{4,3,2,1,0:T(4,128)S(1)}, f32[3,2,2,4,512]{4,3,2,1,0:T(4,128)S(1)}, u32[]{:S(2)}, u32[]{:S(2)}) %collective-permute-start.4) | collective-permute-done | bytes 98336 | tf_op jit(solution)/shard_map/ppermute | solution.py:24
  46.0 0.6 %copy.17 = f32[2,3,4,511]{3,2,1,0:T(4,128)} copy(f32[2,3,4,511]{3,2,0,1:T(4,128)S(1)} %get-tuple-element.19) | data formatting | bytes 98112
  46.6 0.6 %copy.18 = f32[2,3,4,511]{3,2,1,0:T(4,128)} copy(f32[2,3,4,511]{3,2,0,1:T(4,128)S(1)} %get-tuple-element.18) | data formatting | bytes 98112
  (7 shorter events, 0.1 us)
Async XLA Ops:
  0.6 27.6 %collective-permute-start = (bf16[1,3,542,256]{3,2,1,0:T(8,128)(2,1)}, bf16[1,3,542,256]{3,2,1,0:T(8,128)(2,1)S(1)}, u32[]{:S(2)}, u32[]{:S(2)}) collective-permute-start(bf16[1,3,542,256]{3,2,1,0:T(8,128)(2,1)} %w_own.1), channel_id=1, source_target_pairs={{0,16},{16,0},{1,17},{17,1},{2,18},{18,2},{3,19},{19,3},{4,20},{20... | collective-permute-start | bytes 2497544 | tf_op jit(solution)/shard_map/ppermute | solution.py:24
  4.4 4.2 %collective-permute-start.1 = (bf16[1,2,2,3,4,512]{5,4,3,2,1,0:T(4,128)(2,1)S(1)}, bf16[1,2,2,3,4,512]{5,4,3,2,1,0:T(4,128)(2,1)S(1)}, u32[]{:S(2)}, u32[]{:S(2)}) collective-permute-start(bf16[1,2,2,3,4,512]{5,4,3,2,1,0:T(4,128)(2,1)S(1)} %fusion.3.refs_0_), channel_id=1, source_target_pairs={{0,1},{1,0},{2,3},{3,2},{4,5},{5,4},{6,7},{7,6},{8,9},{9,8},{10,11... | collective-permute-start | bytes 147464 | tf_op jit(solution)/shard_map/ppermute | solution.py:24
  8.7 6.8 %collective-permute-start.2 = (bf16[2,2,2,3,4,512]{5,4,3,2,1,0:T(4,128)(2,1)S(1)}, bf16[2,2,2,3,4,512]{5,4,3,2,1,0:T(4,128)(2,1)S(1)}, u32[]{:S(2)}, u32[]{:S(2)}) collective-permute-start(bf16[2,2,2,3,4,512]{5,4,3,2,1,0:T(4,128)(2,1)S(1)} %pad_maximum_fusion), channel_id=1, source_target_pairs={{0,2},{1,3},{2,0},{3,1},{4,6},{5,7},{6,4},{7,5},{8,10},{9,11},{10,... | collective-permute-start | bytes 294920 | tf_op jit(solution)/shard_map/ppermute | solution.py:24
  15.5 1.2 %copy-start.1 = (bf16[1,3,542,256]{3,2,1,0:T(8,128)(2,1)S(1)}, bf16[1,3,542,256]{3,2,1,0:T(8,128)(2,1)}, u32[]{:S(2)}) copy-start(bf16[1,3,542,256]{3,2,1,0:T(8,128)(2,1)} %w_own.1) | copy-start | bytes 2497540
  25.5 2.7 %copy-start = (bf16[3,1,2,128,4096]{4,3,2,1,0:T(8,128)(2,1)}, bf16[3,1,2,128,4096]{4,3,2,1,0:T(8,128)(2,1)S(1)}, u32[]{:S(2)}) copy-start(bf16[3,1,2,128,4096]{4,3,2,1,0:T(8,128)(2,1)S(1)} %get-tuple-element.7.refs_1_) | copy-start | bytes 18874372
  39.9 4.7 %collective-permute-start.3 = (f32[3,2,2,4,512]{4,3,2,1,0:T(4,128)S(1)}, f32[3,2,2,4,512]{4,3,2,1,0:T(4,128)S(1)}, u32[]{:S(2)}, u32[]{:S(2)}) collective-permute-start(f32[3,2,2,4,512]{4,3,2,1,0:T(4,128)S(1)} %back.1), channel_id=1, source_target_pairs={{0,8},{4,12},{8,0},{12,4},{1,9},{5,13},{9,1},{13,5},{2,10},{6,14},... | collective-permute-start | bytes 294920 | tf_op jit(solution)/shard_map/ppermute | solution.py:24
  44.6 1.4 %collective-permute-start.4 = (f32[3,2,2,4,512]{4,3,2,1,0:T(4,128)S(1)}, f32[3,2,2,4,512]{4,3,2,1,0:T(4,128)S(1)}, u32[]{:S(2)}, u32[]{:S(2)}) collective-permute-start(f32[3,2,2,4,512]{4,3,2,1,0:T(4,128)S(1)} %add.40), channel_id=1, source_target_pairs={{0,4},{4,0},{8,12},{12,8},{1,5},{5,1},{9,13},{13,9},{2,6},{6,2},{1... | collective-permute-start | bytes 294920 | tf_op jit(solution)/shard_map/ppermute | solution.py:24

commit v2 on v0

v2 whole, which is shorter than its diff:
```python
import functools

import jax
import jax.numpy as jnp
from jax import lax
from jax.experimental import pallas as pl
from jax.experimental.pallas import tpu as pltpu
from jax.sharding import PartitionSpec as P

TILE = 16
BF = jnp.bfloat16
F32 = jnp.float32


def mm(a, b):
    return jnp.dot(a, b, preferred_element_type=F32)


def split(v):
    high = v.astype(BF)
    return high, (v - high.astype(F32)).astype(BF)


def exchange(cells, axis, step):
    count = lax.axis_size(axis)
    return lax.ppermute(cells, axis, [(i, i ^ step) for i in range(count)])


def fill(dst, at, cells):
    rows, width = cells.shape
    depth = dst.shape[0]
    whole = rows // 16 * 16
    dst[whole:depth, at : at + width] = jnp.zeros((depth - whole, width), BF)
    dst[0:rows, at : at + width] = cells


def below(side, j, x):
    left = (j > x).astype(jnp.int32)
    right = (j < x).astype(jnp.int32)
    return (side * left + (1 - side) * right) > 0


def front(dims, scalars, w_ref, *refs):
    count, own, colours, n_nb, tiles, width, strip, rows, height, ranks = dims
    kern = refs[:count]
    band_nb, cols, pred = refs[count : count + 3]
    if own:
        cat_own, cat_nb, v_own = refs[count + 3 : count + 6]
    wp, band, vl, masks = refs[-4:]
    lanes = 2 * strip
    depth = wp.shape[0]
    groups = width // 16
    wide = lanes // width
    for n in range(n_nb):
        for t in range(tiles):
            j = lax.broadcasted_iota(jnp.int32, (strip, width), 0)
            x = lax.broadcasted_iota(jnp.int32, (strip, width), 1) + t * width
            masks[n, t] = below(scalars[tiles + n], j, x).astype(F32).astype(BF)

    @pl.loop(0, colours)
    def _(q):
        fill(wp, 0, w_ref[0, q])
        for t in range(tiles):
            pick = scalars[t]
            for p in range(count):
                row_taps = kern[p][0, pick, q].astype(F32)
                col_taps = kern[p][1, pick, q].astype(F32)
                col_taps = jnp.concatenate(
                    [col_taps, jnp.zeros((ranks, depth - lanes), F32)], axis=1
                )
                for r in range(ranks):
                    slot = p * ranks + r
                    one = jnp.broadcast_to(row_taps[r : r + 1], (16, lanes))
                    base = pltpu.roll(one, 0, 1, stride=1, stride_axis=0).astype(BF)
                    for b in range(groups):
                        turned = base if b == 0 else pltpu.roll(base, 16 * b, 1)
                        for a in range(wide):
                            at = (t - a) % wide * width
                            tile = turned[:, at : at + width]
                            j = 16 * (groups * a + b)
                            if j < strip:
                                for n in range(n_nb):
                                    kept = tile * masks[n, t, j : j + 16, :]
                                    first = slot * strip + j
                                    band_nb[q, n, t, first : first + 16, :] = kept
                                    if own:
                                        side = (t * ranks + r) * width
                                        cat_nb[q, n, j : j + 16, side : side + width] = kept
                            else:
                                j -= strip
                                first = slot * strip + j
                                band[first : first + 16, :] = tile
                                if own:
                                    side = (t * ranks + r) * width
                                    cat_own[q, j : j + 16, side : side + width] = tile
                    one = jnp.broadcast_to(col_taps[r : r + 1], (16, depth))
                    base = pltpu.roll(one, 0, 1, stride=1, stride_axis=0).astype(BF)
                    for b in range(height // 16):
                        first = slot * height + 16 * b
                        turned = base if b == 0 else pltpu.roll(base, 16 * b, 1)
                        cols[q, t, first : first + 16, :] = turned
            v = mm(cols[q, t], wp[...])
            high, low = split(v)
            for r in range(count * ranks):
                span = slice(r * height, (r + 1) * height)
                vl[:, r * strip : (r + 1) * strip] = high[span]
                if own:
                    v_own[q, t, r, 0:height, :] = high[span]
                    v_own[q, t, r, height : 2 * height, :] = low[span]
            pred[q, t] = mm(vl[...], band[...])


def fold(rows):
    lanes = rows.shape[1]
    total = rows[0:8]
    for g in range(1, rows.shape[0] // 8):
        total = total + pltpu.roll(rows[8 * g : 8 * g + 8], lanes - 8 * g, 1)
    return total


def settle(acc):
    count, lanes = acc.shape
    sub = lax.broadcasted_iota(jnp.int32, acc.shape, 0)
    for bit in (1, 2, 4):
        acc = jnp.where((sub & bit) != 0, pltpu.roll(acc, lanes - bit, 1), acc)
    return jnp.sum(acc.reshape(count // 8, 8, lanes), axis=1)


def back(dims, scalars, w_own, meas, keep, *refs):
    q, n_nb, groups, tiles, width, strip, rows, height, ranks, scale = dims
    halos = refs[:n_nb]
    at = n_nb
    parts = []
    for _ in range(groups):
        parts.append(refs[at : at + 3])
        at += 3
    cat_own, cat_nb, v_own = refs[at : at + 3]
    out, wp, vl, vn, spread, us, acc, acc_z = refs[at + 3 :]
    lanes = 2 * strip
    for n in range(n_nb):
        fill(wp, n * strip, halos[n][0, 0])
    fill(wp, n_nb * strip, w_own[0, q])
    block = lax.broadcasted_iota(jnp.int32, (width, width), 1) // height
    per = width // height
    for t in range(tiles):
        total = jnp.zeros((height, width), F32)
        for i, (bands, cols, pred) in enumerate(parts):
            total = total + pred[q, t]
            count = bands.shape[3] // strip
            for n in range(n_nb):
                v = mm(cols[q, t], wp[:, n * strip : (n + 1) * strip])
                high, low = split(v)
                for r in range(count):
                    span = slice(r * height, (r + 1) * height)
                    vl[:, r * strip : (r + 1) * strip] = high[span]
                    if i == 0:
                        vn[n, r, 0:height, :] = high[span]
                        vn[n, r, height : 2 * height, :] = low[span]
                total = total + mm(vl[:, : count * strip], bands[q, n, t])
        cut = slice(t * width, (t + 1) * width)
        residual = keep[:, cut] * (total - meas[0, q, :, cut].astype(F32))
        residual = residual.astype(BF).astype(F32)
        turned = jnp.transpose(jnp.concatenate([residual] * per, axis=0)).astype(BF)
        pair = turned[:, : 2 * height]
        x = lax.broadcasted_iota(jnp.int32, (width, strip), 0) + t * width
        j = lax.broadcasted_iota(jnp.int32, (width, strip), 1)
        for r in range(ranks):
            near = mm(pair, v_own[q, t, r])
            far = jnp.zeros((width, strip), F32)
            for n in range(n_nb):
                mask = below(scalars[tiles + n], j, x)
                far = far + jnp.where(mask, mm(pair, vn[n, r]), 0.0)
            i = t * ranks + r
            acc[8 * i : 8 * i + 8, :] = pltpu.roll(
                fold(jnp.concatenate([far, near], axis=1)), lanes - (t * width + 1), 1
            )
            for c in range(tiles * ranks // per):
                hit = block + c * per == i
                spread[i * width : (i + 1) * width, c * width : (c + 1) * width] = jnp.where(
                    hit, turned.astype(F32), 0.0
                ).astype(BF)
    for n in range(n_nb + 1):
        cat = cat_own[q] if n == n_nb else cat_nb[q, n]
        high, low = split(mm(cat, spread[...]))
        us[0, n * strip : (n + 1) * strip, :] = high
        us[1, n * strip : (n + 1) * strip, :] = low
    z = jnp.transpose(mm(wp[...], us[0]) + mm(wp[...], us[1]))
    for i in range(tiles * ranks):
        acc_z[8 * i : 8 * i + 8, :] = fold(z[i * height : (i + 1) * height])
    row_grads = settle(acc[...]) * scale
    col_grads = settle(acc_z[...])[:, :lanes] * scale
    for s in range(tiles):
        row = jnp.zeros((ranks, lanes), F32)
        col = jnp.zeros((ranks, lanes), F32)
        for t in range(tiles):
            hit = scalars[t] == s
            span = slice(t * ranks, (t + 1) * ranks)
            row = row + jnp.where(hit, row_grads[span], 0.0)
            col = col + jnp.where(hit, col_grads[span], 0.0)
        out[0, s] = row
        out[1, s] = col


def body(pattern, measured, row_kernels, col_kernels, tile_patch, sat_tiles):
    _, colours, rows, strip = pattern.shape
    height = measured.shape[2]
    tiles, _, ranks, taps = row_kernels.shape
    width = strip // tiles
    lanes = 2 * strip
    depth = -(-rows // 128) * 128
    fields = lax.axis_size("field")
    banks = lax.axis_size("bank")
    caps = lax.axis_size("cap")
    here = lax.axis_index("field")

    rest = ((0, 0),) * 3 + ((0, lanes - taps),)
    kern = jnp.stack([jnp.flip(jnp.pad(row_kernels, rest), 3), jnp.pad(col_kernels, rest)])

    halos = []
    for q in range(colours):
        part = pattern[:, q : q + 1]
        if fields == 2:
            halos.append([exchange(part, "field", 1)])
        else:
            right = [(i, i + 1) for i in range(fields - 1)]
            left = [(i + 1, i) for i in range(fields - 1)]
            halos.append([lax.ppermute(part, "field", right), lax.ppermute(part, "field", left)])
    sides = [here] if fields == 2 else [jnp.ones_like(here), jnp.zeros_like(here)]
    n_nb = len(sides)
    scalars = jnp.concatenate([tile_patch, jnp.stack(sides).astype(jnp.int32)])

    others = [exchange(kern, "bank", k) for k in range(1, banks)]
    pieces = [[kern], others[:1], others[1:]]

    strip_tiles = strip // TILE
    across = strip_tiles * fields
    row_ids = jnp.arange(height // TILE, dtype=jnp.int32)
    col_ids = here * strip_tiles + jnp.arange(strip_tiles, dtype=jnp.int32)
    tile_ids = row_ids[:, None] * across + col_ids[None, :]
    saturated = jnp.any(tile_ids[:, :, None] == sat_tiles[0][None, None, :], axis=-1)
    keep = 1.0 - saturated.astype(F32)
    keep = jnp.broadcast_to(
        keep[:, None, :, None], (height // TILE, TILE, strip_tiles, TILE)
    ).reshape(height, strip)

    vmem = pltpu.VMEM
    smem = pl.BlockSpec(memory_space=pltpu.SMEM)
    whole = pl.BlockSpec(memory_space=pltpu.VMEM)
    params = pltpu.CompilerParams(vmem_limit_bytes=24 * 2**20)
    cells = tiles * ranks

    fronts = []
    extras = None
    for i, piece in enumerate(pieces):
        own = i == 0
        held = len(piece) * ranks
        shapes = [
            ((colours, n_nb, tiles, held * strip, width), BF),
            ((colours, tiles, held * height, depth), BF),
            ((colours, tiles, height, width), F32),
        ]
        if own:
            shapes += [
                ((colours, strip, cells * width), BF),
                ((colours, n_nb, strip, cells * width), BF),
                ((colours, tiles, ranks, 2 * height, strip), BF),
            ]
        dims = (len(piece), own, colours, n_nb, tiles, width, strip, rows, height, ranks)
        got = pl.pallas_call(
            functools.partial(front, dims),
            in_specs=[smem] + [whole] * (1 + len(piece)),
            out_specs=[whole] * len(shapes),
            out_shape=[jax.ShapeDtypeStruct(s, d) for s, d in shapes],
            scratch_shapes=[
                vmem((depth, strip), BF),
                vmem((held * strip, width), BF),
                vmem((height, held * strip), BF),
                vmem((n_nb, tiles, strip, width), BF),
            ],
            compiler_params=params,
            cost_estimate=pl.CostEstimate(
                flops=2 * 10**8 * len(piece), bytes_accessed=4 * 10**6, transcendentals=0
            ),
            name=f"front{i}",
        )(scalars, pattern, *piece)
        fronts += got[:3]
        if own:
            extras = got[3:]

    grads = []
    for q in range(colours):
        dims = (q, n_nb, len(pieces), tiles, width, strip, rows, height, ranks, 1.0 / height)
        most = max(len(p) for p in pieces) * ranks
        grads.append(
            pl.pallas_call(
                functools.partial(back, dims),
                in_specs=[smem] + [whole] * (3 + n_nb + len(fronts) + len(extras)),
                out_specs=whole,
                out_shape=jax.ShapeDtypeStruct((2, tiles, ranks, lanes), F32),
                scratch_shapes=[
                    vmem((depth, (n_nb + 1) * strip), BF),
                    vmem((height, most * strip), BF),
                    vmem((n_nb, ranks, 2 * height, strip), BF),
                    vmem((cells * width, cells * height), BF),
                    vmem((2, (n_nb + 1) * strip, cells * height), BF),
                    vmem((8 * cells, lanes), F32),
                    vmem((8 * cells, depth), F32),
                ],
                compiler_params=params,
                cost_estimate=pl.CostEstimate(
                    flops=10**9, bytes_accessed=4 * 10**6, transcendentals=0
                ),
                name=f"back{q}",
            )(scalars, pattern, measured, keep, *halos[q], *fronts, *extras)
        )
    grads = jnp.stack(grads, axis=2)
    step = caps // 2
    while step:
        grads = grads + exchange(grads, "cap", step)
        step //= 2
    grads = grads[..., :taps]
    return grads[0], grads[1]


def solution(mesh):
    return jax.shard_map(
        body,
        mesh=mesh,
        in_specs=(
            P("cap", None, None, "field"),
            P("cap", None, None, "field"),
            P("field", None, "bank", None),
            P("field", None, "bank", None),
            P("field"),
            P("cap", None),
        ),
        out_specs=(P("field", None, "bank", None), P("field", None, "bank", None)),
        check_vma=False,
    )
```

time: 206 us -> 48.7 us (0.24)
  local copies, waits for them, and re-layouts: 78.3 us -> 4.67 us
  waiting for transfers between devices: 51.5 us -> 4.4 us
  Pallas kernels: 0 us -> 26.9 us
  matrix products: 22.8 us -> 0 us
  other arithmetic: 17.2 us -> 0.49 us
  between operations: 14.4 us -> 0.83 us
  blocking collectives: 13.3 us -> 0 us
  starting transfers between devices: 7.13 us -> 11.2 us
    reshape x12 -> x1, local copies, waits for them, and re-layouts: 48.3 us -> 0.15 us  [body(): keep = jnp.broadcast_to(keep[:, None, :, None], (height // TILE, TILE, st...]
    psum x1 -> x0, waiting for transfers between devices: 30 us -> none  [body(): summed_rows, summed_cols = lax.psum((row_total, col_total), 'cap')]
    pallas_call x0 -> x6, Pallas kernels: none -> 26.9 us  [the longest x3 14.4 us: body(): pl.pallas_call(functools.partial(back, dims), in_specs=[smem] + [whole] *...]
    dot_general x12 -> x0, matrix products: 22.8 us -> none  [the longest x2 12.5 us: body(): jnp.einsum('cqrkx,cqkj->qrxj', backward, windows[tile_index], preferred_e...]
    reduce_scatter x1 -> x0, waiting for transfers between devices: 21.4 us -> none  [body(): lax.psum_scatter(partial_value, 'bank', scatter_dimension=2, tiled=True)]
    slice x10 -> x1, local copies, waits for them, and re-layouts: 15.3 us -> 1.18 us  [body(): part = pattern[:, q:q + 1]]
    all_gather x1 -> x0, blocking collectives: 13.3 us -> none  [body(): residual = lax.all_gather(residual_rows, 'bank', axis=2, tiled=True)]
    another operation x9 -> x1, local copies, waits for them, and re-layouts: 12.5 us -> 0.75 us  [body(): jnp.stack([jnp.flip(jnp.pad(row_kernels, rest), 3), jnp.pad(col_kernels,...]
  transfers between devices with their start and end apart: 4 -> 8, of which waited for: 2 -> 2; matrix products, arithmetic and copies ran while one was open for 16% -> 4% of each run, Pallas kernels for 0% -> 45%
where the time goes in v2:
time: 48.7 us; the launch traced here: 48.5 us
  Pallas kernels  26.9 us (55%)
  starting transfers between devices  11.2 us (23%)
  local copies, waits for them, and re-layouts  4.67 us (10%)
  waiting for transfers between devices  4.4 us (9%)
  between operations  0.83 us (2%)
  other arithmetic  0.49 us (1%)
    pallas_call x3, Pallas kernels, body(): pl.pallas_call(functools.partial(back, dims), in_specs=[smem] + [whole] *...  14.4 us
    pallas_call x3, Pallas kernels, body(): pl.pallas_call(functools.partial(front, dims), in_specs=[smem] + [whole]...  12.4 us
    ppermute x8, starting transfers between devices, exchange(): return lax.ppermute(cells, axis, [(i, i ^ step) for i in range(count)])  11.2 us
    ppermute x8, waiting for transfers between devices, exchange(): return lax.ppermute(cells, axis, [(i, i ^ step) for i in range(count)])  4.4 us
    unnamed x10, local copies, waits for them, and re-layouts  1.27 us
    slice x1, local copies, waits for them, and re-layouts, body(): part = pattern[:, q:q + 1]  1.18 us
  transfers between devices with their start and end apart: 8, of which 2 were waited for; matrix products, arithmetic and copies ran while one was open for 4% of the time, Pallas kernels for 45%

profile of v2, /device:TPU:0, one launch (start us, length us, event | category | flops | bytes accessed | tf_op | source)
XLA Modules:
  0.0 48.5 jit_solution(10249317180706181488)
XLA Ops:
  0.6 0.0 copy-start
  0.6 0.0 copy-start.2
  0.7 0.0 copy-start.3
  0.7 0.8 %pad.7 = bf16[2,3,4,512]{3,2,1,0:T(4,128)(2,1)S(1)} pad(bf16[2,3,4,511]{3,2,1,0:T(4,128)(2,1)} %param.8, bf16[]{:T(256)} %constant.16.clone.1), padding=0_0x0_0x0_0x0_1 | pad | bytes 49106 | tf_op jit(solution)/shard_map/jit(_pad)/pad | solution.py:217
  1.5 0.4 rev.4
  1.9 0.8 %pad_bitcast_fusion = bf16[1,2,3,4,512]{4,3,2,1,0:T(4,128)(2,1)S(1)} fusion(bf16[2,3,4,511]{3,2,1,0:T(4,128)(2,1)} %param.9), kind=kLoop, calls=%fused_computation.5 | loop fusion | bytes 49104 | tf_op jit(solution)/shard_map/stack | solution.py:217
  2.7 5.1 %collective-permute-start.3 = (bf16[2,2,3,4,512]{4,3,2,1,0:T(4,128)(2,1)S(1)}, bf16[2,2,3,4,512]{4,3,2,1,0:T(4,128)(2,1)S(1)}, u32[]{:S(2)}, u32[]{:S(2)}) collective-permute-start(bf16[2,2,3,4,512]{4,3,2,1,0:T(4,128)(2,1)S(1)} %pad_maximum_fusion.1.refs_0_), channel_id=1, source_target_pairs={{0,3},{1,2},{2,1},{3,0},{4,7},{5,6},{6,5},{7,4},{8,11},{9,10},{10,... | collective-permute-start | bytes 147464 | tf_op jit(solution)/shard_map/ppermute | solution.py:26
  7.8 0.0 collective-permute-start.2
  7.9 0.6 %collective-permute-start.1 = (bf16[2,2,3,4,512]{4,3,2,1,0:T(4,128)(2,1)S(1)}, bf16[2,2,3,4,512]{4,3,2,1,0:T(4,128)(2,1)S(1)}, u32[]{:S(2)}, u32[]{:S(2)}) collective-permute-start(bf16[2,2,3,4,512]{4,3,2,1,0:T(4,128)(2,1)S(1)} %pad_maximum_fusion.1.refs_0_), channel_id=1, source_target_pairs={{0,1},{1,0},{2,3},{3,2},{4,5},{5,4},{6,7},{7,6},{8,9},{9,8},{10,11... | collective-permute-start | bytes 147464 | tf_op jit(solution)/shard_map/ppermute | solution.py:26
  8.5 1.2 %fusion.1 = (bf16[1,1,542,256]{3,2,1,0:T(8,128)(2,1)S(1)}, bf16[1,1,542,256]{3,2,1,0:T(8,128)(2,1)S(1)}, bf16[1,1,542,256]{3,2,1,0:T(8,128)(2,1)S(1)}) fusion(bf16[1,3,542,256]{3,2,1,0:T(8,128)(2,1)} %w_own.5), kind=kLoop, calls=%fused_computation.12 | loop fusion | bytes 1665024 | tf_op jit(solution)/shard_map/slice | solution.py:221
  9.7 1.7 %collective-permute-start = (bf16[1,1,542,256]{3,2,1,0:T(8,128)(2,1)S(1)}, bf16[1,1,542,256]{3,2,1,0:T(8,128)(2,1)S(1)}, u32[]{:S(2)}, u32[]{:S(2)}) collective-permute-start(bf16[1,1,542,256]{3,2,1,0:T(8,128)(2,1)S(1)} %get-tuple-element.30), channel_id=1, source_target_pairs={{0,16},{16,0},{1,17},{17,1},{2,18},{18,2},{3,19},{19,3},{4,20},{20... | collective-permute-start | bytes 832520 | tf_op jit(solution)/shard_map/ppermute | solution.py:26
  11.4 0.4 collective-permute-start.5
  11.8 0.1 broadcast_add_fusion
  11.8 0.0 copy-done.2
  11.8 0.2 compare_reduce_fusion
  12.0 0.0 collective-permute-done.1.refs_0_
  12.1 1.7 %collective-permute-start.4 = (bf16[1,1,542,256]{3,2,1,0:T(8,128)(2,1)S(1)}, bf16[1,1,542,256]{3,2,1,0:T(8,128)(2,1)S(1)}, u32[]{:S(2)}, u32[]{:S(2)}) collective-permute-start(bf16[1,1,542,256]{3,2,1,0:T(8,128)(2,1)S(1)} %get-tuple-element.31), channel_id=1, source_target_pairs={{0,16},{16,0},{1,17},{17,1},{2,18},{18,2},{3,19},{19,3},{4,20},{20... | collective-permute-start | bytes 832520 | tf_op jit(solution)/shard_map/ppermute | solution.py:26
  13.8 0.0 copy-done.3
  13.8 0.1 pad_add_fusion.scalars
  13.8 0.1 broadcast_in_dim.2
  13.9 0.1 reshape.48.keep
  14.1 0.0 copy-done
  14.1 0.0 copy-start.1
  14.1 3.5 %front0.1 = (bf16[3,1,2,1024,128]{4,3,2,1,0:T(8,128)(2,1)S(1)}, bf16[3,2,128,640]{3,2,1,0:T(8,128)(2,1)S(1)}, f32[3,2,32,128]{3,2,1,0:T(8,128)S(1)}, bf16[3,256,...) custom-call(s32[3]{0:T(128)S(1)} %pad_add_fusion.scalars, ...), custom_call_target="tpu_custom_call" | custom-call | flops 200000000 | bytes 4000000 | tf_op jit(solution)/shard_map/front0/pallas_call | solution.py:269
  17.6 3.5 %front1.1 = (bf16[3,1,2,1024,128]{4,3,2,1,0:T(8,128)(2,1)S(1)}, bf16[3,2,128,640]{3,2,1,0:T(8,128)(2,1)S(1)}, f32[3,2,32,128]{3,2,1,0:T(8,128)S(1)}) custom-call(s32[3]{0:T(128)S(1)} %pad_add_fusion.scalars, bf16[1,3,542,256]{3,2,1,0:T(8,128)(2,1)S(1)} %copy-done, bf16[2,2,3,4,512]{4,3,2,1,0:T(4,128)(2,1)S(1)} %collective-permute-done.1.refs_0_), custom_call_target="tpu_custom_call" | custom-call | flops 200000000 | bytes 4000000 | tf_op jit(solution)/shard_map/front1/pallas_call | solution.py:269
  21.1 0.0 collective-permute-done.3.refs_1_
  21.1 0.0 collective-permute-done.2.refs_0_
  21.1 5.4 %front2.1 = (bf16[3,1,2,2048,128]{4,3,2,1,0:T(8,128)(2,1)S(1)}, bf16[3,2,256,640]{3,2,1,0:T(8,128)(2,1)S(1)}, f32[3,2,32,128]{3,2,1,0:T(8,128)S(1)}) custom-call(s32[3]{0:T(128)S(1)} %pad_add_fusion.scalars, bf16[1,3,542,256]{3,2,1,0:T(8,128)(2,1)S(1)} %copy-done, bf16[2,2,3,4,512]{4,3,2,1,0:T(4,128)(2,1)S(1)} %collective-permute-done.2.refs_0_, ...), custom_call_target="tpu_custom_call" | custom-call | flops 400000000 | bytes 4000000 | tf_op jit(solution)/shard_map/front2/pallas_call | solution.py:269
  26.6 0.0 collective-permute-done.5.refs_0_
  26.6 0.0 copy-done.1
  26.6 4.8 %back2.1 = f32[2,2,4,512]{3,2,1,0:T(4,128)S(1)} custom-call(s32[3]{0:T(128)S(1)} %pad_add_fusion.scalars, bf16[1,3,542,256]{3,2,1,0:T(8,128)(2,1)S(1)} %copy-done, bf16[1,3,32,256]{3,2,1,0:T(8,128)(2,1)S(1)} %copy-done.1, f32[32,256]{1,0:T(8,128)S(1)} %reshape.48.keep, bf16[1,1,542,256]{3,2,1,0:T(8,128)(2,1)S(1)} %collective-permute-done.5.refs_0_, ...), custom_call_target="tpu_custom_call" | custom-call | flops 1000000000 | bytes 4000000 | tf_op jit(solution)/shard_map/back2/pallas_call | solution.py:295
  31.4 0.0 collective-permute-done.4.refs_0_
  31.4 4.8 %back1.1 = f32[2,2,4,512]{3,2,1,0:T(4,128)S(1)} custom-call(s32[3]{0:T(128)S(1)} %pad_add_fusion.scalars, bf16[1,3,542,256]{3,2,1,0:T(8,128)(2,1)S(1)} %copy-done, bf16[1,3,32,256]{3,2,1,0:T(8,128)(2,1)S(1)} %copy-done.1, f32[32,256]{1,0:T(8,128)S(1)} %reshape.48.keep, bf16[1,1,542,256]{3,2,1,0:T(8,128)(2,1)S(1)} %collective-permute-done.4.refs_0_, ...), custom_call_target="tpu_custom_call" | custom-call | flops 1000000000 | bytes 4000000 | tf_op jit(solution)/shard_map/back1/pallas_call | solution.py:295
  36.2 0.0 collective-permute-done.refs_0_
  36.2 4.8 %back0.1 = f32[2,2,4,512]{3,2,1,0:T(4,128)S(1)} custom-call(s32[3]{0:T(128)S(1)} %pad_add_fusion.scalars, bf16[1,3,542,256]{3,2,1,0:T(8,128)(2,1)S(1)} %copy-done, bf16[1,3,32,256]{3,2,1,0:T(8,128)(2,1)S(1)} %copy-done.1, f32[32,256]{1,0:T(8,128)S(1)} %reshape.48.keep, bf16[1,1,542,256]{3,2,1,0:T(8,128)(2,1)S(1)} %collective-permute-done.refs_0_, ...), custom_call_target="tpu_custom_call" | custom-call | flops 1000000000 | bytes 4000000 | tf_op jit(solution)/shard_map/back0/pallas_call | solution.py:295
  41.1 1.6 %collective-permute-start.6 = (f32[2,2,3,4,512]{4,3,1,0,2:T(4,128)S(1)}, f32[2,2,3,4,512]{4,3,1,0,2:T(4,128)S(1)}, u32[]{:S(2)}, u32[]{:S(2)}) collective-permute-start(f32[2,2,3,4,512]{4,3,1,0,2:T(4,128)S(1)} %pad_maximum_fusion), channel_id=1, source_target_pairs={{0,8},{4,12},{8,0},{12,4},{1,9},{5,13},{9,1},{13,5},{2,10},{6,14},... | collective-permute-start | bytes 294920 | tf_op jit(solution)/shard_map/ppermute | solution.py:26
  42.7 3.1 %collective-permute-done.6 = f32[2,2,3,4,512]{4,3,1,0,2:T(4,128)S(1)} collective-permute-done((f32[2,2,3,4,512]{4,3,1,0,2:T(4,128)S(1)}, f32[2,2,3,4,512]{4,3,1,0,2:T(4,128)S(1)}, u32[]{:S(2)}, u32[]{:S(2)}) %collective-permute-start.6) | collective-permute-done | bytes 98336 | tf_op jit(solution)/shard_map/ppermute | solution.py:26
  45.8 0.1 collective-permute-start.7
  45.9 1.3 %collective-permute-done.7 = f32[2,2,3,4,512]{4,3,1,0,2:T(4,128)S(1)} collective-permute-done((f32[2,2,3,4,512]{4,3,1,0,2:T(4,128)S(1)}, f32[2,2,3,4,512]{4,3,1,0,2:T(4,128)S(1)}, u32[]{:S(2)}, u32[]{:S(2)}) %collective-permute-start.7) | collective-permute-done | bytes 98336 | tf_op jit(solution)/shard_map/ppermute | solution.py:26
  47.2 0.6 %copy.11 = f32[2,3,4,511]{3,2,1,0:T(4,128)} copy(f32[2,3,4,511]{3,2,0,1:T(4,128)S(1)} %get-tuple-element.33) | data formatting | bytes 98112
  47.9 0.6 %copy.10 = f32[2,3,4,511]{3,2,1,0:T(4,128)} copy(f32[2,3,4,511]{3,2,0,1:T(4,128)S(1)} %get-tuple-element.34) | data formatting | bytes 98112
  (8 shorter events, 0.2 us)
Async XLA Ops:
  0.6 13.4 %copy-start = (bf16[1,3,542,256]{3,2,1,0:T(8,128)(2,1)S(1)}, bf16[1,3,542,256]{3,2,1,0:T(8,128)(2,1)}, u32[]{:S(2)}) copy-start(bf16[1,3,542,256]{3,2,1,0:T(8,128)(2,1)} %w_own.5) | copy-start | bytes 2497540
  0.6 11.2 %copy-start.2 = (s32[1,256]{1,0:T(1,128)S(1)}, s32[1,256]{1,0:T(1,128)}, u32[]{:S(2)}) copy-start(s32[1,256]{1,0:T(1,128)} %param.11) | copy-start | bytes 3076
  0.7 13.1 %copy-start.3 = (s32[2]{0:T(128)S(1)}, s32[2]{0:T(128)}, u32[]{:S(2)}) copy-start(s32[2]{0:T(128)} %param.10) | copy-start | bytes 28
  2.7 18.4 %collective-permute-start.3 = (bf16[2,2,3,4,512]{4,3,2,1,0:T(4,128)(2,1)S(1)}, bf16[2,2,3,4,512]{4,3,2,1,0:T(4,128)(2,1)S(1)}, u32[]{:S(2)}, u32[]{:S(2)}) collective-permute-start(bf16[2,2,3,4,512]{4,3,2,1,0:T(4,128)(2,1)S(1)} %pad_maximum_fusion.1.refs_0_), channel_id=1, source_target_pairs={{0,3},{1,2},{2,1},{3,0},{4,7},{5,6},{6,5},{7,4},{8,11},{9,10},{10,... | collective-permute-start | bytes 147464 | tf_op jit(solution)/shard_map/ppermute | solution.py:26
  7.8 13.3 %collective-permute-start.2 = (bf16[2,2,3,4,512]{4,3,2,1,0:T(4,128)(2,1)S(1)}, bf16[2,2,3,4,512]{4,3,2,1,0:T(4,128)(2,1)S(1)}, u32[]{:S(2)}, u32[]{:S(2)}) collective-permute-start(bf16[2,2,3,4,512]{4,3,2,1,0:T(4,128)(2,1)S(1)} %pad_maximum_fusion.1.refs_0_), channel_id=1, source_target_pairs={{0,2},{1,3},{2,0},{3,1},{4,6},{5,7},{6,4},{7,5},{8,10},{9,11},{10,... | collective-permute-start | bytes 147464 | tf_op jit(solution)/shard_map/ppermute | solution.py:26
  7.9 4.2 %collective-permute-start.1 = (bf16[2,2,3,4,512]{4,3,2,1,0:T(4,128)(2,1)S(1)}, bf16[2,2,3,4,512]{4,3,2,1,0:T(4,128)(2,1)S(1)}, u32[]{:S(2)}, u32[]{:S(2)}) collective-permute-start(bf16[2,2,3,4,512]{4,3,2,1,0:T(4,128)(2,1)S(1)} %pad_maximum_fusion.1.refs_0_), channel_id=1, source_target_pairs={{0,1},{1,0},{2,3},{3,2},{4,5},{5,4},{6,7},{7,6},{8,9},{9,8},{10,11... | collective-permute-start | bytes 147464 | tf_op jit(solution)/shard_map/ppermute | solution.py:26
  9.7 26.6 %collective-permute-start = (bf16[1,1,542,256]{3,2,1,0:T(8,128)(2,1)S(1)}, bf16[1,1,542,256]{3,2,1,0:T(8,128)(2,1)S(1)}, u32[]{:S(2)}, u32[]{:S(2)}) collective-permute-start(bf16[1,1,542,256]{3,2,1,0:T(8,128)(2,1)S(1)} %get-tuple-element.30), channel_id=1, source_target_pairs={{0,16},{16,0},{1,17},{17,1},{2,18},{18,2},{3,19},{19,3},{4,20},{20... | collective-permute-start | bytes 832520 | tf_op jit(solution)/shard_map/ppermute | solution.py:26
  11.4 15.2 %collective-permute-start.5 = (bf16[1,1,542,256]{3,2,1,0:T(8,128)(2,1)S(1)}, bf16[1,1,542,256]{3,2,1,0:T(8,128)(2,1)S(1)}, u32[]{:S(2)}, u32[]{:S(2)}) collective-permute-start(bf16[1,1,542,256]{3,2,1,0:T(8,128)(2,1)S(1)} %get-tuple-element.32), channel_id=1, source_target_pairs={{0,16},{16,0},{1,17},{17,1},{2,18},{18,2},{3,19},{19,3},{4,20},{20... | collective-permute-start | bytes 832520 | tf_op jit(solution)/shard_map/ppermute | solution.py:26
  12.1 19.4 %collective-permute-start.4 = (bf16[1,1,542,256]{3,2,1,0:T(8,128)(2,1)S(1)}, bf16[1,1,542,256]{3,2,1,0:T(8,128)(2,1)S(1)}, u32[]{:S(2)}, u32[]{:S(2)}) collective-permute-start(bf16[1,1,542,256]{3,2,1,0:T(8,128)(2,1)S(1)} %get-tuple-element.31), channel_id=1, source_target_pairs={{0,16},{16,0},{1,17},{17,1},{2,18},{18,2},{3,19},{19,3},{4,20},{20... | collective-permute-start | bytes 832520 | tf_op jit(solution)/shard_map/ppermute | solution.py:26
  14.1 12.5 %copy-start.1 = (bf16[1,3,32,256]{3,2,1,0:T(8,128)(2,1)S(1)}, bf16[1,3,32,256]{3,2,1,0:T(8,128)(2,1)}, u32[]{:S(2)}) copy-start(bf16[1,3,32,256]{3,2,1,0:T(8,128)(2,1)} %meas.5) | copy-start | bytes 147460
  41.1 4.7 %collective-permute-start.6 = (f32[2,2,3,4,512]{4,3,1,0,2:T(4,128)S(1)}, f32[2,2,3,4,512]{4,3,1,0,2:T(4,128)S(1)}, u32[]{:S(2)}, u32[]{:S(2)}) collective-permute-start(f32[2,2,3,4,512]{4,3,1,0,2:T(4,128)S(1)} %pad_maximum_fusion), channel_id=1, source_target_pairs={{0,8},{4,12},{8,0},{12,4},{1,9},{5,13},{9,1},{13,5},{2,10},{6,14},... | collective-permute-start | bytes 294920 | tf_op jit(solution)/shard_map/ppermute | solution.py:26
  45.8 1.4 %collective-permute-start.7 = (f32[2,2,3,4,512]{4,3,1,0,2:T(4,128)S(1)}, f32[2,2,3,4,512]{4,3,1,0,2:T(4,128)S(1)}, u32[]{:S(2)}, u32[]{:S(2)}) collective-permute-start(f32[2,2,3,4,512]{4,3,1,0,2:T(4,128)S(1)} %fusion), channel_id=1, source_target_pairs={{0,4},{4,0},{8,12},{12,8},{1,5},{5,1},{9,13},{13,9},{2,6},{6,2},{1... | collective-permute-start | bytes 294920 | tf_op jit(solution)/shard_map/ppermute | solution.py:26

commit v3 on v2

v3 whole, which is shorter than its diff:
```python
import functools

import jax
import jax.numpy as jnp
from jax import lax
from jax.experimental import pallas as pl
from jax.experimental.pallas import tpu as pltpu
from jax.sharding import PartitionSpec as P

TILE = 16
BF = jnp.bfloat16
F32 = jnp.float32


def mm(a, b):
    return jnp.dot(a, b, preferred_element_type=F32)


def mt(a, b):
    return lax.dot_general(a, b, (((1,), (1,)), ((), ())), preferred_element_type=F32)


def split(v):
    high = v.astype(BF)
    return high, (v - high.astype(F32)).astype(BF)


def exchange(cells, axis, step):
    count = lax.axis_size(axis)
    return lax.ppermute(cells, axis, [(i, i ^ step) for i in range(count)])


def fill(dst, at, cells):
    rows, width = cells.shape
    depth = dst.shape[0]
    whole = rows // 16 * 16
    dst[whole:depth, at : at + width] = jnp.zeros((depth - whole, width), BF)
    dst[0:rows, at : at + width] = cells


def below(side, j, x):
    left = (j > x).astype(jnp.int32)
    right = (j < x).astype(jnp.int32)
    return (side * left + (1 - side) * right) > 0


def front(dims, scalars, w_ref, *refs):
    count, colours, n_nb, tiles, width, strip, rows, height, ranks = dims
    kern = refs[:count]
    band_nb, band_own, cols, v_own, pred, wp, vl, masks = refs[count:]
    lanes = 2 * strip
    depth = wp.shape[0]
    held = count * ranks
    for n in range(n_nb):
        for t in range(tiles):
            x = lax.broadcasted_iota(jnp.int32, (width, strip), 0) + t * width
            j = lax.broadcasted_iota(jnp.int32, (width, strip), 1)
            masks[n, t] = below(scalars[tiles + n], j, x).astype(F32).astype(BF)

    @pl.loop(0, colours)
    def _(q):
        fill(wp, 0, w_ref[0, q])
        for t in range(tiles):
            pick = scalars[t]
            for p in range(count):
                taps = kern[p][1, pick, q].astype(F32)
                taps = jnp.concatenate([taps, jnp.zeros((ranks, depth - lanes), F32)], axis=1)
                for r in range(ranks):
                    first = (p * ranks + r) * height
                    one = jnp.broadcast_to(taps[r : r + 1], (height, depth)).astype(BF)
                    cols[q, t, first : first + height, :] = pltpu.roll(
                        one, 0, 1, stride=1, stride_axis=0
                    )
            v = mm(cols[q, t], wp[...])
            vl[t] = v.astype(BF)
            for r in range(ranks):
                high, low = split(v[r * height : (r + 1) * height])
                v_own[q, t, r, 0:height, :] = high
                v_own[q, t, r, height : 2 * height, :] = low
        for t in range(tiles):
            pick = scalars[t]
            total = jnp.zeros((height, width), F32)
            for p in range(count):
                taps = kern[p][0, pick, q].astype(F32)
                for r in range(ranks):
                    slot = p * ranks + r
                    at = slot * strip
                    one = jnp.broadcast_to(taps[r : r + 1], (width, lanes)).astype(BF)
                    tile = pltpu.roll(one, 1 + t * width, 1, stride=1, stride_axis=0)
                    for n in range(n_nb):
                        band_nb[q, n, t, :, at : at + strip] = tile[:, :strip] * masks[n, t]
                    if p == 0:
                        band_own[q, t, :, at : at + strip] = tile[:, strip:]
                    total = total + mt(
                        vl[t, slot * height : (slot + 1) * height, :], tile[:, strip:]
                    )
            pred[q, t] = total


def fold(rows):
    lanes = rows.shape[1]
    total = rows[0:8]
    for g in range(1, rows.shape[0] // 8):
        total = total + pltpu.roll(rows[8 * g : 8 * g + 8], lanes - 8 * g, 1)
    return total


def settle(acc):
    blocks, count, wide = acc.shape
    total = None
    for i in reversed(range(8)):
        rows = jnp.concatenate(
            [acc[c, pl.ds(i, count // 8, stride=8), :] for c in range(blocks)], axis=1
        )
        if total is None:
            total = rows
        else:
            total = pltpu.roll(total, blocks * wide - 1, 1) + rows
    return total


def keep_in(acc, first, rows):
    for c in range(acc.shape[0]):
        acc[c, first : first + rows.shape[0], :] = rows[:, c * 128 : (c + 1) * 128]


def back(dims, scalars, w_own, meas, keep, *refs):
    q, n_nb, held, tiles, width, strip, rows, height, ranks, scale = dims
    halos = refs[:n_nb]
    band_nb, band_own, cols, v_own, pred, out, wp, vl, vn, us, acc, acc_z = refs[n_nb:]
    lanes = 2 * strip
    near = ranks * strip
    cells = tiles * ranks
    for n in range(n_nb):
        fill(wp, n * strip, halos[n][0, 0])
    fill(wp, n_nb * strip, w_own[0, q])
    for n in range(n_nb):
        for t in range(tiles):
            v = mm(cols[q, t], wp[:, n * strip : (n + 1) * strip])
            vl[n, t] = v.astype(BF)
            for r in range(ranks):
                high, low = split(v[r * height : (r + 1) * height])
                vn[n, t, r, 0:height, :] = high
                vn[n, t, r, height : 2 * height, :] = low
    for t in range(tiles):
        total = pred[q, t]
        for n in range(n_nb):
            for r in range(held):
                total = total + mt(
                    vl[n, t, r * height : (r + 1) * height, :],
                    band_nb[q, n, t, :, r * strip : (r + 1) * strip],
                )
        cut = slice(t * width, (t + 1) * width)
        residual = keep[:, cut] * (total - meas[0, q, :, cut].astype(F32))
        residual = residual.astype(BF)
        wide = residual.astype(F32)
        pair = jnp.transpose(jnp.concatenate([wide] * (width // height), axis=0)).astype(BF)
        pair = pair[:, : 2 * height]
        x = lax.broadcasted_iota(jnp.int32, (width, strip), 0) + t * width
        j = lax.broadcasted_iota(jnp.int32, (width, strip), 1)
        for n in range(n_nb + 1):
            bands = band_own[q, t] if n == n_nb else band_nb[q, n, t, :, :near]
            high, low = split(mm(residual, bands))
            for r in range(ranks):
                first = (t * ranks + r) * height
                take = slice(r * strip, (r + 1) * strip)
                span = slice(n * strip, (n + 1) * strip)
                us[first : first + height, span] = high[:, take]
                us[cells * height + first : cells * height + first + height, span] = low[:, take]
        for r in range(ranks):
            far = jnp.zeros((width, strip), F32)
            for n in range(n_nb):
                mask = below(scalars[tiles + n], j, x)
                far = far + jnp.where(mask, mm(pair, vn[n, t, r]), 0.0)
            both = jnp.concatenate([far, mm(pair, v_own[q, t, r])], axis=1)
            part = pltpu.roll(fold(both), lanes - (t * width + 1), 1)
            keep_in(acc, 8 * (t * ranks + r), part)
    z = mt(us[...], wp[...])
    z = z[: cells * height] + z[cells * height :]
    for i in range(cells):
        keep_in(acc_z, 8 * i, fold(z[i * height : (i + 1) * height]))
    row_grads = settle(acc) * scale
    col_grads = settle(acc_z)[:, :lanes] * scale
    for s in range(tiles):
        row = jnp.zeros((ranks, lanes), F32)
        col = jnp.zeros((ranks, lanes), F32)
        for t in range(tiles):
            hit = scalars[t] == s
            span = slice(t * ranks, (t + 1) * ranks)
            row = row + jnp.where(hit, row_grads[span], 0.0)
            col = col + jnp.where(hit, col_grads[span], 0.0)
        out[0, s] = row
        out[1, s] = col


def body(pattern, measured, row_kernels, col_kernels, tile_patch, sat_tiles):
    _, colours, rows, strip = pattern.shape
    height = measured.shape[2]
    tiles, _, ranks, taps = row_kernels.shape
    width = strip // tiles
    lanes = 2 * strip
    depth = -(-rows // 128) * 128
    fields = lax.axis_size("field")
    banks = lax.axis_size("bank")
    caps = lax.axis_size("cap")
    here = lax.axis_index("field")

    rest = ((0, 0),) * 3 + ((0, lanes - taps),)
    kern = jnp.pad(jnp.stack([row_kernels, col_kernels]), ((0, 0),) + rest)

    halos = []
    for q in range(colours):
        part = pattern[:, q : q + 1]
        if fields == 2:
            halos.append([exchange(part, "field", 1)])
        else:
            right = [(i, i + 1) for i in range(fields - 1)]
            left = [(i + 1, i) for i in range(fields - 1)]
            halos.append([lax.ppermute(part, "field", right), lax.ppermute(part, "field", left)])
    sides = [here] if fields == 2 else [jnp.ones_like(here), jnp.zeros_like(here)]
    n_nb = len(sides)
    scalars = jnp.concatenate([tile_patch, jnp.stack(sides).astype(jnp.int32)])

    pieces = [kern] + [exchange(kern, "bank", k) for k in range(1, banks)]

    strip_tiles = strip // TILE
    across = strip_tiles * fields
    row_ids = jnp.arange(height // TILE, dtype=jnp.int32)
    col_ids = here * strip_tiles + jnp.arange(strip_tiles, dtype=jnp.int32)
    tile_ids = row_ids[:, None] * across + col_ids[None, :]
    saturated = jnp.any(tile_ids[:, :, None] == sat_tiles[0][None, None, :], axis=-1)
    keep = 1.0 - saturated.astype(F32)
    keep = jnp.broadcast_to(
        keep[:, None, :, None], (height // TILE, TILE, strip_tiles, TILE)
    ).reshape(height, strip)

    vmem = pltpu.VMEM
    smem = pl.BlockSpec(memory_space=pltpu.SMEM)
    whole = pl.BlockSpec(memory_space=pltpu.VMEM)
    params = pltpu.CompilerParams(vmem_limit_bytes=24 * 2**20)
    cells = tiles * ranks

    held = len(pieces) * ranks
    shapes = [
        ((colours, n_nb, tiles, width, held * strip), BF),
        ((colours, tiles, width, ranks * strip), BF),
        ((colours, tiles, held * height, depth), BF),
        ((colours, tiles, ranks, 2 * height, strip), BF),
        ((colours, tiles, height, width), F32),
    ]
    fronts = pl.pallas_call(
        functools.partial(
            front, (len(pieces), colours, n_nb, tiles, width, strip, rows, height, ranks)
        ),
        in_specs=[smem] + [whole] * (1 + len(pieces)),
        out_specs=[whole] * len(shapes),
        out_shape=[jax.ShapeDtypeStruct(s, d) for s, d in shapes],
        scratch_shapes=[
            vmem((depth, strip), BF),
            vmem((tiles, held * height, strip), BF),
            vmem((n_nb, tiles, width, strip), BF),
        ],
        compiler_params=params,
        cost_estimate=pl.CostEstimate(
            flops=2 * 10**9, bytes_accessed=4 * 10**6, transcendentals=0
        ),
        name="front",
    )(scalars, pattern, *pieces)

    grads = []
    for q in range(colours):
        dims = (q, n_nb, held, tiles, width, strip, rows, height, ranks, 1.0 / height)
        grads.append(
            pl.pallas_call(
                functools.partial(back, dims),
                in_specs=[smem] + [whole] * (3 + n_nb + len(fronts)),
                out_specs=whole,
                out_shape=jax.ShapeDtypeStruct((2, tiles, ranks, lanes), F32),
                scratch_shapes=[
                    vmem((depth, (n_nb + 1) * strip), BF),
                    vmem((n_nb, tiles, held * height, strip), BF),
                    vmem((n_nb, tiles, ranks, 2 * height, strip), BF),
                    vmem((2 * cells * height, (n_nb + 1) * strip), BF),
                    vmem((lanes // 128, 8 * cells, 128), F32),
                    vmem((depth // 128, 8 * cells, 128), F32),
                ],
                compiler_params=params,
                cost_estimate=pl.CostEstimate(
                    flops=10**9, bytes_accessed=4 * 10**6, transcendentals=0
                ),
                name=f"back{q}",
            )(scalars, pattern, measured, keep, *halos[q], *fronts)
        )
    grads = jnp.stack(grads, axis=2)
    step = caps // 2
    while step:
        grads = grads + exchange(grads, "cap", step)
        step //= 2
    grads = grads[..., :taps]
    return grads[0], grads[1]


def solution(mesh):
    return jax.shard_map(
        body,
        mesh=mesh,
        in_specs=(
            P("cap", None, None, "field"),
            P("cap", None, None, "field"),
            P("field", None, "bank", None),
            P("field", None, "bank", None),
            P("field"),
            P("cap", None),
        ),
        out_specs=(P("field", None, "bank", None), P("field", None, "bank", None)),
        check_vma=False,
    )
```

time: 48.7 us -> 44.4 us (0.912)
  Pallas kernels: 26.9 us -> 17.8 us
  waiting for transfers between devices: 4.4 us -> 7.86 us
  other arithmetic: 0.49 us -> 2.57 us
  local copies, waits for them, and re-layouts: 4.67 us -> 3.82 us
    pallas_call x3 -> x1, Pallas kernels: 12.4 us -> 5.1 us  [body(): pl.pallas_call(functools.partial(front, (len(pieces), colours, n_nb, tile...]
    ppermute x8, waiting for transfers between devices: 4.4 us -> 7.86 us  [exchange(): return lax.ppermute(cells, axis, [(i, i ^ step) for i in range(count)])]
    pallas_call x3, Pallas kernels: 14.4 us -> 12.7 us  [body(): pl.pallas_call(functools.partial(back, dims), in_specs=[smem] + [whole] *...]
    unnamed x10 -> x6, local copies, waits for them, and re-layouts: 1.27 us -> 2.4 us
    pad x1 -> x0, local copies, waits for them, and re-layouts: 0.83 us -> none  [body(): jnp.pad(row_kernels, rest)]
    another operation x1 -> x0, local copies, waits for them, and re-layouts: 0.75 us -> none  [body(): jnp.stack([jnp.flip(jnp.pad(row_kernels, rest), 3), jnp.pad(col_kernels,...]
    another operation x1, other arithmetic: 0.04 us -> 0.79 us  [body(): kern = jnp.pad(jnp.stack([row_kernels, col_kernels]), ((0, 0),) + rest)]
    reduce_or x1, other arithmetic: 0.18 us -> 0.86 us  [body(): jnp.any(tile_ids[:, :, None] == sat_tiles[0][None, None, :], axis=-1)]
  transfers between devices with their start and end apart: 8 -> 8, of which waited for: 2 -> 3; matrix products, arithmetic and copies ran while one was open for 4% -> 7% of each run, Pallas kernels for 45% -> 31%
where the time goes in v3:
time: 44.4 us; the launch traced here: 44.1 us
  Pallas kernels  17.8 us (40%)
  starting transfers between devices  11.4 us (26%)
  waiting for transfers between devices  7.86 us (18%)
  local copies, waits for them, and re-layouts  3.82 us (9%)
  other arithmetic  2.57 us (6%)
  between operations  0.74 us (2%)
    pallas_call x3, Pallas kernels, body(): pl.pallas_call(functools.partial(back, dims), in_specs=[smem] + [whole] *...  12.7 us
    ppermute x8, starting transfers between devices, exchange(): return lax.ppermute(cells, axis, [(i, i ^ step) for i in range(count)])  11.4 us
    ppermute x8, waiting for transfers between devices, exchange(): return lax.ppermute(cells, axis, [(i, i ^ step) for i in range(count)])  7.86 us
    pallas_call x1, Pallas kernels, body(): pl.pallas_call(functools.partial(front, (len(pieces), colours, n_nb, tile...  5.1 us
    unnamed x6, local copies, waits for them, and re-layouts  2.4 us
    slice x1, local copies, waits for them, and re-layouts, body(): part = pattern[:, q:q + 1]  1.18 us
  transfers between devices with their start and end apart: 8, of which 3 were waited for; matrix products, arithmetic and copies ran while one was open for 7% of the time, Pallas kernels for 31%

profile of v3, /device:TPU:0, one launch (start us, length us, event | category | flops | bytes accessed | tf_op | source)
XLA Modules:
  0.0 44.1 jit_solution(9759377488486986072)
XLA Ops:
  0.6 0.8 %fusion.2.refs_0_ = bf16[2,2,3,4,512]{4,3,2,1,0:T(4,128)(2,1)S(1)} fusion(bf16[1,2,3,4,511]{4,3,2,1,0:T(4,128)(2,1)} %bitcast.22, bf16[1,2,3,4,511]{4,3,2,1,0:T(4,128)(2,1)} %bitcast.23), kind=kLoop, calls=%fused_computation.4 | loop fusion | flops 172032 | bytes 98208 | tf_op jit(solution)/shard_map/stack | solution.py:209
  1.4 5.1 %collective-permute-start.3 = (bf16[2,2,3,4,512]{4,3,2,1,0:T(4,128)(2,1)S(1)}, bf16[2,2,3,4,512]{4,3,2,1,0:T(4,128)(2,1)S(1)}, u32[]{:S(2)}, u32[]{:S(2)}) collective-permute-start(bf16[2,2,3,4,512]{4,3,2,1,0:T(4,128)(2,1)S(1)} %fusion.2.refs_0_), channel_id=1, source_target_pairs={{0,3},{1,2},{2,1},{3,0},{4,7},{5,6},{6,5},{7,4},{8,11},{9,10},{10,... | collective-permute-start | bytes 147464 | tf_op jit(solution)/shard_map/ppermute | solution.py:30
  6.6 0.0 collective-permute-start.2
  6.6 0.6 %collective-permute-start.1 = (bf16[2,2,3,4,512]{4,3,2,1,0:T(4,128)(2,1)S(1)}, bf16[2,2,3,4,512]{4,3,2,1,0:T(4,128)(2,1)S(1)}, u32[]{:S(2)}, u32[]{:S(2)}) collective-permute-start(bf16[2,2,3,4,512]{4,3,2,1,0:T(4,128)(2,1)S(1)} %fusion.2.refs_0_), channel_id=1, source_target_pairs={{0,1},{1,0},{2,3},{3,2},{4,5},{5,4},{6,7},{7,6},{8,9},{9,8},{10,11... | collective-permute-start | bytes 147464 | tf_op jit(solution)/shard_map/ppermute | solution.py:30
  7.2 1.2 %fusion.4 = (bf16[1,1,542,256]{3,2,1,0:T(8,128)(2,1)S(1)}, bf16[1,1,542,256]{3,2,1,0:T(8,128)(2,1)S(1)}, bf16[1,1,542,256]{3,2,1,0:T(8,128)(2,1)S(1)}) fusion(bf16[1,3,542,256]{3,2,1,0:T(8,128)(2,1)} %w_own.5), kind=kLoop, calls=%fused_computation.14 | loop fusion | bytes 1665024 | tf_op jit(solution)/shard_map/slice | solution.py:213
  8.4 1.7 %collective-permute-start = (bf16[1,1,542,256]{3,2,1,0:T(8,128)(2,1)S(1)}, bf16[1,1,542,256]{3,2,1,0:T(8,128)(2,1)S(1)}, u32[]{:S(2)}, u32[]{:S(2)}) collective-permute-start(bf16[1,1,542,256]{3,2,1,0:T(8,128)(2,1)S(1)} %get-tuple-element.16), channel_id=1, source_target_pairs={{0,16},{16,0},{1,17},{17,1},{2,18},{18,2},{3,19},{19,3},{4,20},{20... | collective-permute-start | bytes 832520 | tf_op jit(solution)/shard_map/ppermute | solution.py:30
  10.1 0.4 collective-permute-start.5
  10.5 0.1 broadcast_add_fusion
  10.6 0.9 %compare_reduce_fusion = pred[2,16]{1,0:T(4,128)(4,1)S(1)} fusion(s32[256]{0:T(256)} %bitcast.24, s32[2,16]{1,0:T(2,128)S(1)} %broadcast_add_fusion), kind=kLoop, calls=%fused_computation.7 | loop fusion | flops 16352 | bytes 1184 | tf_op jit(solution)/shard_map/reduce_or | solution.py:231
  11.4 0.7 %pad_add_fusion.scalars = s32[3]{0:T(128)S(1)} fusion(s32[1]{0:T(128)} %bitcast, s32[2]{0:T(128)} %param.10), kind=kLoop, calls=%fused_computation.9 | loop fusion | flops 3 | bytes 24 | tf_op jit(solution)/shard_map/concatenate | solution.py:222
  12.2 0.0 copy-start.1
  12.2 0.1 broadcast_in_dim.2
  12.3 0.1 reshape.48.keep
  12.4 0.0 collective-permute-done.3.refs_3_
  12.4 1.7 %collective-permute-start.4 = (bf16[1,1,542,256]{3,2,1,0:T(8,128)(2,1)S(1)}, bf16[1,1,542,256]{3,2,1,0:T(8,128)(2,1)S(1)}, u32[]{:S(2)}, u32[]{:S(2)}) collective-permute-start(bf16[1,1,542,256]{3,2,1,0:T(8,128)(2,1)S(1)} %get-tuple-element.17), channel_id=1, source_target_pairs={{0,16},{16,0},{1,17},{17,1},{2,18},{18,2},{3,19},{19,3},{4,20},{20... | collective-permute-start | bytes 832520 | tf_op jit(solution)/shard_map/ppermute | solution.py:30
  14.1 0.0 collective-permute-done.2.refs_2_
  14.1 0.0 collective-permute-done.1.refs_1_
  14.1 0.0 copy-start
  14.1 1.1 %copy-done = bf16[1,3,542,256]{3,2,1,0:T(8,128)(2,1)S(1)} copy-done((bf16[1,3,542,256]{3,2,1,0:T(8,128)(2,1)S(1)}, bf16[1,3,542,256]{3,2,1,0:T(8,128)(2,1)}, u32[]{:S(2)}) %copy-start) | copy-done | bytes 832536
  15.3 5.1 %front.1 = (bf16[3,1,2,128,4096]{4,3,2,1,0:T(8,128)(2,1)S(1)}, bf16[3,2,128,1024]{3,2,1,0:T(8,128)(2,1)S(1)}, bf16[3,2,512,640]{3,2,1,0:T(8,128)(2,1)S(1)}, bf16...) custom-call(s32[3]{0:T(128)S(1)} %pad_add_fusion.scalars, bf16[1,3,542,256]{3,2,1,0:T(8,128)(2,1)S(1)} %copy-done, ...), custom_call_target="tpu_custom_call" | custom-call | flops 2000000000 | bytes 4000000 | tf_op jit(solution)/shard_map/front/pallas_call | solution.py:251
  20.4 3.6 %collective-permute-done.5.refs_0_ = bf16[1,1,542,256]{3,2,1,0:T(8,128)(2,1)S(1)} collective-permute-done((bf16[1,1,542,256]{3,2,1,0:T(8,128)(2,1)S(1)}, bf16[1,1,542,256]{3,2,1,0:T(8,128)(2,1)S(1)}, u32[]{:S(2)}, u32[]{:S(2)}) %collective-permute-start.5) | collective-permute-done | bytes 277536 | tf_op jit(solution)/shard_map/ppermute | solution.py:30
  24.0 0.0 copy-done.1
  24.0 4.2 %back2.1 = f32[2,2,4,512]{3,2,1,0:T(4,128)S(1)} custom-call(s32[3]{0:T(128)S(1)} %pad_add_fusion.scalars, bf16[1,3,542,256]{3,2,1,0:T(8,128)(2,1)S(1)} %copy-done, bf16[1,3,32,256]{3,2,1,0:T(8,128)(2,1)S(1)} %copy-done.1, f32[32,256]{1,0:T(8,128)S(1)} %reshape.48.keep, bf16[1,1,542,256]{3,2,1,0:T(8,128)(2,1)S(1)} %collective-permute-done.5.refs_0_, ...), custom_call_target="tpu_custom_call" | custom-call | flops 1000000000 | bytes 4000000 | tf_op jit(solution)/shard_map/back2/pallas_call | solution.py:274
  28.2 0.0 collective-permute-done.4.refs_0_
  28.2 4.2 %back1.1 = f32[2,2,4,512]{3,2,1,0:T(4,128)S(1)} custom-call(s32[3]{0:T(128)S(1)} %pad_add_fusion.scalars, bf16[1,3,542,256]{3,2,1,0:T(8,128)(2,1)S(1)} %copy-done, bf16[1,3,32,256]{3,2,1,0:T(8,128)(2,1)S(1)} %copy-done.1, f32[32,256]{1,0:T(8,128)S(1)} %reshape.48.keep, bf16[1,1,542,256]{3,2,1,0:T(8,128)(2,1)S(1)} %collective-permute-done.4.refs_0_, ...), custom_call_target="tpu_custom_call" | custom-call | flops 1000000000 | bytes 4000000 | tf_op jit(solution)/shard_map/back1/pallas_call | solution.py:274
  32.5 0.0 collective-permute-done.refs_0_
  32.5 4.2 %back0.1 = f32[2,2,4,512]{3,2,1,0:T(4,128)S(1)} custom-call(s32[3]{0:T(128)S(1)} %pad_add_fusion.scalars, bf16[1,3,542,256]{3,2,1,0:T(8,128)(2,1)S(1)} %copy-done, bf16[1,3,32,256]{3,2,1,0:T(8,128)(2,1)S(1)} %copy-done.1, f32[32,256]{1,0:T(8,128)S(1)} %reshape.48.keep, bf16[1,1,542,256]{3,2,1,0:T(8,128)(2,1)S(1)} %collective-permute-done.refs_0_, ...), custom_call_target="tpu_custom_call" | custom-call | flops 1000000000 | bytes 4000000 | tf_op jit(solution)/shard_map/back0/pallas_call | solution.py:274
  36.7 1.7 %collective-permute-start.6 = (f32[2,2,3,4,512]{4,3,1,0,2:T(4,128)S(1)}, f32[2,2,3,4,512]{4,3,1,0,2:T(4,128)S(1)}, u32[]{:S(2)}, u32[]{:S(2)}) collective-permute-start(f32[2,2,3,4,512]{4,3,1,0,2:T(4,128)S(1)} %pad_maximum_fusion), channel_id=1, source_target_pairs={{0,8},{4,12},{8,0},{12,4},{1,9},{5,13},{9,1},{13,5},{2,10},{6,14},... | collective-permute-start | bytes 294920 | tf_op jit(solution)/shard_map/ppermute | solution.py:30
  38.5 3.0 %collective-permute-done.6 = f32[2,2,3,4,512]{4,3,1,0,2:T(4,128)S(1)} collective-permute-done((f32[2,2,3,4,512]{4,3,1,0,2:T(4,128)S(1)}, f32[2,2,3,4,512]{4,3,1,0,2:T(4,128)S(1)}, u32[]{:S(2)}, u32[]{:S(2)}) %collective-permute-start.6) | collective-permute-done | bytes 98336 | tf_op jit(solution)/shard_map/ppermute | solution.py:30
  41.5 0.1 collective-permute-start.7
  41.5 1.3 %collective-permute-done.7 = f32[2,2,3,4,512]{4,3,1,0,2:T(4,128)S(1)} collective-permute-done((f32[2,2,3,4,512]{4,3,1,0,2:T(4,128)S(1)}, f32[2,2,3,4,512]{4,3,1,0,2:T(4,128)S(1)}, u32[]{:S(2)}, u32[]{:S(2)}) %collective-permute-start.7) | collective-permute-done | bytes 98336 | tf_op jit(solution)/shard_map/ppermute | solution.py:30
  42.9 0.6 %copy.11 = f32[2,3,4,511]{3,2,1,0:T(4,128)} copy(f32[2,3,4,511]{3,2,0,1:T(4,128)S(1)} %get-tuple-element.19) | data formatting | bytes 98112
  43.5 0.6 %copy.10 = f32[2,3,4,511]{3,2,1,0:T(4,128)} copy(f32[2,3,4,511]{3,2,0,1:T(4,128)S(1)} %get-tuple-element.20) | data formatting | bytes 98112
  (7 shorter events, 0.1 us)
Async XLA Ops:
  1.4 11.0 %collective-permute-start.3 = (bf16[2,2,3,4,512]{4,3,2,1,0:T(4,128)(2,1)S(1)}, bf16[2,2,3,4,512]{4,3,2,1,0:T(4,128)(2,1)S(1)}, u32[]{:S(2)}, u32[]{:S(2)}) collective-permute-start(bf16[2,2,3,4,512]{4,3,2,1,0:T(4,128)(2,1)S(1)} %fusion.2.refs_0_), channel_id=1, source_target_pairs={{0,3},{1,2},{2,1},{3,0},{4,7},{5,6},{6,5},{7,4},{8,11},{9,10},{10,... | collective-permute-start | bytes 147464 | tf_op jit(solution)/shard_map/ppermute | solution.py:30
  6.6 7.6 %collective-permute-start.2 = (bf16[2,2,3,4,512]{4,3,2,1,0:T(4,128)(2,1)S(1)}, bf16[2,2,3,4,512]{4,3,2,1,0:T(4,128)(2,1)S(1)}, u32[]{:S(2)}, u32[]{:S(2)}) collective-permute-start(bf16[2,2,3,4,512]{4,3,2,1,0:T(4,128)(2,1)S(1)} %fusion.2.refs_0_), channel_id=1, source_target_pairs={{0,2},{1,3},{2,0},{3,1},{4,6},{5,7},{6,4},{7,5},{8,10},{9,11},{10,... | collective-permute-start | bytes 147464 | tf_op jit(solution)/shard_map/ppermute | solution.py:30
  6.6 7.6 %collective-permute-start.1 = (bf16[2,2,3,4,512]{4,3,2,1,0:T(4,128)(2,1)S(1)}, bf16[2,2,3,4,512]{4,3,2,1,0:T(4,128)(2,1)S(1)}, u32[]{:S(2)}, u32[]{:S(2)}) collective-permute-start(bf16[2,2,3,4,512]{4,3,2,1,0:T(4,128)(2,1)S(1)} %fusion.2.refs_0_), channel_id=1, source_target_pairs={{0,1},{1,0},{2,3},{3,2},{4,5},{5,4},{6,7},{7,6},{8,9},{9,8},{10,11... | collective-permute-start | bytes 147464 | tf_op jit(solution)/shard_map/ppermute | solution.py:30
  8.4 24.1 %collective-permute-start = (bf16[1,1,542,256]{3,2,1,0:T(8,128)(2,1)S(1)}, bf16[1,1,542,256]{3,2,1,0:T(8,128)(2,1)S(1)}, u32[]{:S(2)}, u32[]{:S(2)}) collective-permute-start(bf16[1,1,542,256]{3,2,1,0:T(8,128)(2,1)S(1)} %get-tuple-element.16), channel_id=1, source_target_pairs={{0,16},{16,0},{1,17},{17,1},{2,18},{18,2},{3,19},{19,3},{4,20},{20... | collective-permute-start | bytes 832520 | tf_op jit(solution)/shard_map/ppermute | solution.py:30
  10.1 13.9 %collective-permute-start.5 = (bf16[1,1,542,256]{3,2,1,0:T(8,128)(2,1)S(1)}, bf16[1,1,542,256]{3,2,1,0:T(8,128)(2,1)S(1)}, u32[]{:S(2)}, u32[]{:S(2)}) collective-permute-start(bf16[1,1,542,256]{3,2,1,0:T(8,128)(2,1)S(1)} %get-tuple-element.18), channel_id=1, source_target_pairs={{0,16},{16,0},{1,17},{17,1},{2,18},{18,2},{3,19},{19,3},{4,20},{20... | collective-permute-start | bytes 832520 | tf_op jit(solution)/shard_map/ppermute | solution.py:30
  12.2 11.8 %copy-start.1 = (bf16[1,3,32,256]{3,2,1,0:T(8,128)(2,1)S(1)}, bf16[1,3,32,256]{3,2,1,0:T(8,128)(2,1)}, u32[]{:S(2)}) copy-start(bf16[1,3,32,256]{3,2,1,0:T(8,128)(2,1)} %meas.5) | copy-start | bytes 147460
  12.4 15.8 %collective-permute-start.4 = (bf16[1,1,542,256]{3,2,1,0:T(8,128)(2,1)S(1)}, bf16[1,1,542,256]{3,2,1,0:T(8,128)(2,1)S(1)}, u32[]{:S(2)}, u32[]{:S(2)}) collective-permute-start(bf16[1,1,542,256]{3,2,1,0:T(8,128)(2,1)S(1)} %get-tuple-element.17), channel_id=1, source_target_pairs={{0,16},{16,0},{1,17},{17,1},{2,18},{18,2},{3,19},{19,3},{4,20},{20... | collective-permute-start | bytes 832520 | tf_op jit(solution)/shard_map/ppermute | solution.py:30
  14.1 1.2 %copy-start = (bf16[1,3,542,256]{3,2,1,0:T(8,128)(2,1)S(1)}, bf16[1,3,542,256]{3,2,1,0:T(8,128)(2,1)}, u32[]{:S(2)}) copy-start(bf16[1,3,542,256]{3,2,1,0:T(8,128)(2,1)} %w_own.5) | copy-start | bytes 2497540
  36.7 4.7 %collective-permute-start.6 = (f32[2,2,3,4,512]{4,3,1,0,2:T(4,128)S(1)}, f32[2,2,3,4,512]{4,3,1,0,2:T(4,128)S(1)}, u32[]{:S(2)}, u32[]{:S(2)}) collective-permute-start(f32[2,2,3,4,512]{4,3,1,0,2:T(4,128)S(1)} %pad_maximum_fusion), channel_id=1, source_target_pairs={{0,8},{4,12},{8,0},{12,4},{1,9},{5,13},{9,1},{13,5},{2,10},{6,14},... | collective-permute-start | bytes 294920 | tf_op jit(solution)/shard_map/ppermute | solution.py:30
  41.5 1.4 %collective-permute-start.7 = (f32[2,2,3,4,512]{4,3,1,0,2:T(4,128)S(1)}, f32[2,2,3,4,512]{4,3,1,0,2:T(4,128)S(1)}, u32[]{:S(2)}, u32[]{:S(2)}) collective-permute-start(f32[2,2,3,4,512]{4,3,1,0,2:T(4,128)S(1)} %fusion.3), channel_id=1, source_target_pairs={{0,4},{4,0},{8,12},{12,8},{1,5},{5,1},{9,13},{13,9},{2,6},{6,2},{1... | collective-permute-start | bytes 294920 | tf_op jit(solution)/shard_map/ppermute | solution.py:30

commit v4 on v3

v4 whole, which is shorter than its diff:
```python
import functools

import jax
import jax.numpy as jnp
from jax import lax
from jax.experimental import pallas as pl
from jax.experimental.pallas import tpu as pltpu
from jax.sharding import PartitionSpec as P

TILE = 16
BF = jnp.bfloat16
F32 = jnp.float32


def mm(a, b):
    return jnp.dot(a, b, preferred_element_type=F32)


def mt(a, b):
    return lax.dot_general(a, b, (((1,), (1,)), ((), ())), preferred_element_type=F32)


def split(v):
    high = v.astype(BF)
    return high, (v - high.astype(F32)).astype(BF)


def exchange(cells, axis, step):
    count = lax.axis_size(axis)
    return lax.ppermute(cells, axis, [(i, i ^ step) for i in range(count)])


def fill(dst, at, cells):
    rows, width = cells.shape
    depth = dst.shape[0]
    whole = rows // 16 * 16
    dst[whole:depth, at : at + width] = jnp.zeros((depth - whole, width), BF)
    dst[0:rows, at : at + width] = cells


def below(side, j, x):
    left = (j > x).astype(jnp.int32)
    right = (j < x).astype(jnp.int32)
    return (side * left + (1 - side) * right) > 0


def side_of(n, n_nb, here):
    return here if n_nb == 1 else jnp.int32(1 - n)


def prep(pattern, measured, sat_tiles, row_kernels, col_kernels, *refs):
    colours = pattern.shape[1]
    strips = refs[:colours]
    kern, meas, sat, rows_in, cols_in, rows, cols, sems = refs[colours:]
    tiles, _, ranks, taps = row_kernels.shape
    lanes = rows.shape[1]
    pairs = [(row_kernels, rows_in), (col_kernels, cols_in)]
    pairs += [(pattern.at[:, pl.ds(q, 1)], strips[q]) for q in range(colours)]
    pairs += [(sat_tiles, sat), (measured, meas)]
    copies = [pltpu.make_async_copy(a, b, sems.at[i]) for i, (a, b) in enumerate(pairs)]
    for copy in copies:
        copy.start()
    rows[...] = jnp.zeros(rows.shape, F32)
    cols[...] = jnp.zeros(cols.shape, F32)
    i = lax.broadcasted_iota(jnp.int32, (lanes, lanes), 0)
    m = lax.broadcasted_iota(jnp.int32, (lanes, lanes), 1)
    mirror = (i + m == lanes - 1).astype(F32).astype(BF)
    copies[0].wait()
    copies[1].wait()
    for s in range(tiles):
        for q in range(colours):
            first = (s * colours + q) * ranks
            rows[first : first + ranks, 0:taps] = rows_in[s, q].astype(F32)
            cols[first : first + ranks, 0:taps] = cols_in[s, q].astype(F32)
    mirrored = mm(rows[...].astype(BF), mirror)
    for s in range(tiles):
        for q in range(colours):
            first = (s * colours + q) * ranks
            kern[0, s, q] = mirrored[first : first + ranks].astype(BF)
            kern[1, s, q] = cols[first : first + ranks, :].astype(BF)
    for copy in copies[2:]:
        copy.wait()


def front(dims, tile_patch, sat, *refs):
    count, own, colours, n_nb, tiles, width, strip, rows, height, ranks, fields = dims
    strips = refs[:colours]
    kern = refs[colours : colours + count]
    band_nb, cols, pred = refs[colours + count : colours + count + 3]
    if own:
        band_own, v_own, keep = refs[colours + count + 3 : -5]
    wp, vl, masks, picks, sem = refs[-5:]
    fetch = pltpu.make_async_copy(tile_patch, picks, sem)
    fetch.start()
    lanes = 2 * strip
    depth = wp.shape[0]
    here = lax.axis_index("field")
    for n in range(n_nb):
        side = side_of(n, n_nb, here)
        for t in range(tiles):
            j = lax.broadcasted_iota(jnp.int32, (strip, width), 0)
            x = lax.broadcasted_iota(jnp.int32, (strip, width), 1) + t * width
            masks[n, t] = below(side, j, x).astype(F32).astype(BF)
    if own:
        across = strip // TILE
        boxes = height // TILE * across
        box = lax.broadcasted_iota(jnp.int32, (boxes, 1), 0)
        name = box // across * (across * fields) + here * across + box % across
        hit = jnp.max((sat[...] == name).astype(F32), axis=1, keepdims=True)
        x = lax.broadcasted_iota(jnp.int32, (boxes, strip), 1) // TILE
        wide = jnp.where(x == box % across, hit, 0.0).astype(BF)
        y = lax.broadcasted_iota(jnp.int32, (height, boxes), 0) // TILE
        tall = y == lax.broadcasted_iota(jnp.int32, (height, boxes), 1) // across
        keep[...] = 1.0 - mm(tall.astype(F32).astype(BF), wide)
    fetch.wait()

    for q in range(colours):
        fill(wp, 0, strips[q][0, 0])
        for t in range(tiles):
            pick = picks[t]
            for p in range(count):
                taps = kern[p][1, pick, q].astype(F32)
                taps = jnp.concatenate([taps, jnp.zeros((ranks, depth - lanes), F32)], axis=1)
                for r in range(ranks):
                    first = (p * ranks + r) * height
                    one = jnp.broadcast_to(taps[r : r + 1], (height, depth)).astype(BF)
                    cols[q, t, first : first + height, :] = pltpu.roll(
                        one, 0, 1, stride=1, stride_axis=0
                    )
            v = mm(cols[q, t], wp[...])
            vl[t] = v.astype(BF)
            for r in range(ranks if own else 0):
                high, low = split(v[r * height : (r + 1) * height])
                v_own[q, t, r, 0:height, :] = high
                v_own[q, t, r, height : 2 * height, :] = low
        for t in range(tiles):
            pick = picks[t]
            total = jnp.zeros((height, width), F32)
            for p in range(count):
                taps = kern[p][0, pick, q].astype(F32)
                for r in range(ranks):
                    slot = p * ranks + r
                    at = slot * strip
                    one = jnp.broadcast_to(taps[r : r + 1], (width, lanes)).astype(BF)
                    base = pltpu.roll(one, 0, 1, stride=1, stride_axis=0)
                    blocks = []
                    for a in range(lanes // width):
                        first = (t - a) % (lanes // width) * width
                        blocks.append(base[:, first : first + width])
                    half = len(blocks) // 2
                    for a in range(half):
                        span = slice(a * width, (a + 1) * width)
                        for n in range(n_nb):
                            band_nb[q, n, t, at + a * width : at + (a + 1) * width, :] = (
                                blocks[a] * masks[n, t, span, :]
                            )
                    rest = jnp.concatenate(blocks[half:], axis=0)
                    if own and p == 0:
                        band_own[q, t, at : at + strip, :] = rest
                    total = total + mm(vl[t, slot * height : (slot + 1) * height, :], rest)
            pred[q, t] = total


def fold(rows):
    lanes = rows.shape[1]
    total = rows[0:8]
    for g in range(1, rows.shape[0] // 8):
        total = total + pltpu.roll(rows[8 * g : 8 * g + 8], lanes - 8 * g, 1)
    return total


def settle(acc):
    blocks, count, wide = acc.shape
    total = None
    for i in reversed(range(8)):
        rows = jnp.concatenate(
            [acc[c, pl.ds(i, count // 8, stride=8), :] for c in range(blocks)], axis=1
        )
        if total is None:
            total = rows
        else:
            total = pltpu.roll(total, blocks * wide - 1, 1) + rows
    return total


def keep_in(acc, first, rows):
    for c in range(acc.shape[0]):
        acc[c, first : first + rows.shape[0], :] = rows[:, c * 128 : (c + 1) * 128]


def back(dims, tile_patch, w_own, meas, keep, *refs):
    q, n_nb, parts, tiles, width, strip, rows, height, ranks, scale = dims
    halos = refs[:n_nb]
    fronts = [refs[n_nb + 3 * i : n_nb + 3 * i + 3] for i in range(parts)]
    band_own, v_own, out, wp, vl, vn, us, acc, acc_z, picks, sem = refs[n_nb + 3 * parts :]
    fetch = pltpu.make_async_copy(tile_patch, picks, sem)
    fetch.start()
    lanes = 2 * strip
    near = ranks * strip
    cells = tiles * ranks
    here = lax.axis_index("field")
    for n in range(n_nb):
        fill(wp, n * strip, halos[n][0, 0])
    fill(wp, n_nb * strip, w_own[0, 0])
    for n in range(n_nb):
        for t in range(tiles):
            first = 0
            for i, (_, cols, _) in enumerate(fronts):
                v = mm(cols[q, t], wp[:, n * strip : (n + 1) * strip])
                vl[n, t, first : first + v.shape[0]] = v.astype(BF)
                first += v.shape[0]
                for r in range(ranks if i == 0 else 0):
                    high, low = split(v[r * height : (r + 1) * height])
                    vn[n, t, r, 0:height, :] = high
                    vn[n, t, r, height : 2 * height, :] = low
    pairs = []
    for t in range(tiles):
        total = jnp.zeros((height, width), F32)
        first = 0
        for bands, _, pred in fronts:
            total = total + pred[q, t]
            for r in range(bands.shape[3] // strip):
                for n in range(n_nb):
                    total = total + mm(
                        vl[n, t, first : first + height, :],
                        bands[q, n, t, r * strip : (r + 1) * strip, :],
                    )
                first += height
        cut = slice(t * width, (t + 1) * width)
        residual = keep[:, cut] * (total - meas[0, q, :, cut].astype(F32))
        residual = residual.astype(BF)
        wide = residual.astype(F32)
        pair = jnp.transpose(jnp.concatenate([wide] * (width // height), axis=0)).astype(BF)
        pairs.append(pair[:, : 2 * height])
        for n in range(n_nb + 1):
            bands = band_own[q, t] if n == n_nb else fronts[0][0][q, n, t, :near, :]
            high, low = split(mt(residual, bands))
            for r in range(ranks):
                first = (t * ranks + r) * height
                take = slice(r * strip, (r + 1) * strip)
                span = slice(n * strip, (n + 1) * strip)
                us[first : first + height, span] = high[:, take]
                us[cells * height + first : cells * height + first + height, span] = low[:, take]
    z = mt(us[...], wp[...])
    z = z[: cells * height] + z[cells * height :]
    for t in range(tiles):
        x = lax.broadcasted_iota(jnp.int32, (width, strip), 0) + t * width
        j = lax.broadcasted_iota(jnp.int32, (width, strip), 1)
        for r in range(ranks):
            far = jnp.zeros((width, strip), F32)
            for n in range(n_nb):
                mask = below(side_of(n, n_nb, here), j, x)
                far = far + jnp.where(mask, mm(pairs[t], vn[n, t, r]), 0.0)
            both = jnp.concatenate([far, mm(pairs[t], v_own[q, t, r])], axis=1)
            part = pltpu.roll(fold(both), lanes - (t * width + 1), 1)
            keep_in(acc, 8 * (t * ranks + r), part)
    for i in range(cells):
        keep_in(acc_z, 8 * i, fold(z[i * height : (i + 1) * height]))
    fetch.wait()
    row_grads = settle(acc) * scale
    col_grads = settle(acc_z)[:, :lanes] * scale
    for s in range(tiles):
        row = jnp.zeros((ranks, lanes), F32)
        col = jnp.zeros((ranks, lanes), F32)
        for t in range(tiles):
            hit = picks[t] == s
            span = slice(t * ranks, (t + 1) * ranks)
            row = row + jnp.where(hit, row_grads[span], 0.0)
            col = col + jnp.where(hit, col_grads[span], 0.0)
        out[0, s] = row
        out[1, s] = col


def finish(mine, theirs, rows, cols):
    taps = rows.shape[-1]
    for s in range(rows.shape[0]):
        for q in range(rows.shape[1]):
            rows[s, q] = (mine[0, s, q] + theirs[0, s, q])[:, :taps]
            cols[s, q] = (mine[1, s, q] + theirs[1, s, q])[:, :taps]


def body(pattern, measured, row_kernels, col_kernels, tile_patch, sat_tiles):
    _, colours, rows, strip = pattern.shape
    height = measured.shape[2]
    tiles, _, ranks, taps = row_kernels.shape
    width = strip // tiles
    lanes = 2 * strip
    depth = -(-rows // 128) * 128
    fields = lax.axis_size("field")
    banks = lax.axis_size("bank")
    caps = lax.axis_size("cap")
    cells = tiles * ranks

    vmem = pltpu.VMEM
    hbm = pl.BlockSpec(memory_space=pltpu.HBM)
    whole = pl.BlockSpec(memory_space=pltpu.VMEM)
    params = pltpu.CompilerParams(vmem_limit_bytes=24 * 2**20)

    def cost(flops):
        return pl.CostEstimate(flops=flops, bytes_accessed=4 * 10**6, transcendentals=0)

    pattern, measured, row_kernels, col_kernels, tile_patch, sat_tiles = [
        pltpu.with_memory_space_constraint(array, pltpu.HBM)
        for array in (pattern, measured, row_kernels, col_kernels, tile_patch, sat_tiles)
    ]
    *strips, kern, meas, sat = pl.pallas_call(
        prep,
        in_specs=[hbm] * 5,
        out_specs=[whole] * (colours + 3),
        out_shape=[jax.ShapeDtypeStruct((1, 1, rows, strip), BF)] * colours
        + [
            jax.ShapeDtypeStruct((2, tiles, colours, ranks, lanes), BF),
            jax.ShapeDtypeStruct(measured.shape, measured.dtype),
            jax.ShapeDtypeStruct(sat_tiles.shape, sat_tiles.dtype),
        ],
        scratch_shapes=[
            vmem(row_kernels.shape, BF),
            vmem(col_kernels.shape, BF),
            vmem((tiles * colours * ranks, lanes), F32),
            vmem((tiles * colours * ranks, lanes), F32),
            pltpu.SemaphoreType.DMA((colours + 4,)),
        ],
        compiler_params=params,
        cost_estimate=cost(10**7),
        name="prep",
    )(pattern, measured, sat_tiles, row_kernels, col_kernels)

    halos = []
    for part in strips:
        if fields == 2:
            halos.append([exchange(part, "field", 1)])
        else:
            right = [(i, i + 1) for i in range(fields - 1)]
            left = [(i + 1, i) for i in range(fields - 1)]
            halos.append([lax.ppermute(part, "field", right), lax.ppermute(part, "field", left)])
    n_nb = len(halos[0])
    pieces = [kern] + [exchange(kern, "bank", k) for k in range(1, banks)]
    held = len(pieces) * ranks

    own_shapes = [
        ((colours, tiles, ranks * strip, width), BF),
        ((colours, tiles, ranks, 2 * height, strip), BF),
        ((height, strip), F32),
    ]
    cuts = [pieces[:2], pieces[2:]]
    fronts = []
    for i, cut in enumerate(cuts):
        some = len(cut) * ranks
        shapes = [
            ((colours, n_nb, tiles, some * strip, width), BF),
            ((colours, tiles, some * height, depth), BF),
            ((colours, tiles, height, width), F32),
        ]
        if i == 0:
            shapes += own_shapes
        dims = (len(cut), i == 0, colours, n_nb, tiles, width, strip, rows, height, ranks, fields)
        got = pl.pallas_call(
            functools.partial(front, dims),
            in_specs=[hbm] + [whole] * (1 + colours + len(cut)),
            out_specs=[whole] * len(shapes),
            out_shape=[jax.ShapeDtypeStruct(s, d) for s, d in shapes],
            scratch_shapes=[
                vmem((depth, strip), BF),
                vmem((tiles, some * height, strip), BF),
                vmem((n_nb, tiles, strip, width), BF),
                pltpu.SMEM((tiles,), jnp.int32),
                pltpu.SemaphoreType.DMA,
            ],
            compiler_params=params,
            cost_estimate=cost(10**9),
            name=f"front{i}",
        )(tile_patch, sat, *strips, *cut)
        fronts += got[:3]
        if i == 0:
            band_own, v_own, keep = got[3:]

    grads = []
    for q in range(colours):
        dims = (q, n_nb, len(cuts), tiles, width, strip, rows, height, ranks, 1.0 / height)
        grads.append(
            pl.pallas_call(
                functools.partial(back, dims),
                in_specs=[hbm] + [whole] * (5 + n_nb + len(fronts)),
                out_specs=whole,
                out_shape=jax.ShapeDtypeStruct((2, tiles, ranks, lanes), F32),
                scratch_shapes=[
                    vmem((depth, (n_nb + 1) * strip), BF),
                    vmem((n_nb, tiles, held * height, strip), BF),
                    vmem((n_nb, tiles, ranks, 2 * height, strip), BF),
                    vmem((2 * cells * height, (n_nb + 1) * strip), BF),
                    vmem((lanes // 128, 8 * cells, 128), F32),
                    vmem((depth // 128, 8 * cells, 128), F32),
                    pltpu.SMEM((tiles,), jnp.int32),
                    pltpu.SemaphoreType.DMA,
                ],
                compiler_params=params,
                cost_estimate=cost(10**9),
                name=f"back{q}",
            )(tile_patch, strips[q], meas, keep, *halos[q], *fronts, band_own, v_own)
        )
    grads = jnp.stack(grads, axis=2)
    step = caps // 2
    while step > 1:
        grads = grads + exchange(grads, "cap", step)
        step //= 2
    out = jax.ShapeDtypeStruct((tiles, colours, ranks, taps), F32)
    return pl.pallas_call(
        finish,
        in_specs=[whole] * 2,
        out_specs=[whole] * 2,
        out_shape=[out, out],
        compiler_params=params,
        name="finish",
    )(grads, exchange(grads, "cap", 1))


def solution(mesh):
    return jax.shard_map(
        body,
        mesh=mesh,
        in_specs=(
            P("cap", None, None, "field"),
            P("cap", None, None, "field"),
            P("field", None, "bank", None),
            P("field", None, "bank", None),
            P("field"),
            P("cap", None),
        ),
        out_specs=(P("field", None, "bank", None), P("field", None, "bank", None)),
        check_vma=False,
    )
```

time: 44.4 us -> 34.4 us (0.77)
  local copies, waits for them, and re-layouts: 3.82 us -> 0 us
  waiting for transfers between devices: 7.86 us -> 5.02 us
  other arithmetic: 2.57 us -> 0.06 us
  Pallas kernels: 17.8 us -> 17.3 us
    ppermute x8, waiting for transfers between devices: 7.86 us -> 5.02 us  [exchange(): return lax.ppermute(cells, axis, [(i, i ^ step) for i in range(count)])]
    unnamed x6 -> x0, local copies, waits for them, and re-layouts: 2.4 us -> none
    slice x1 -> x0, local copies, waits for them, and re-layouts: 1.18 us -> none  [body(): part = pattern[:, q:q + 1]]
    reduce_or x1 -> x0, other arithmetic: 0.86 us -> none  [body(): jnp.any(tile_ids[:, :, None] == sat_tiles[0][None, None, :], axis=-1)]
    another operation x1 -> x0, other arithmetic: 0.79 us -> none  [body(): kern = jnp.pad(jnp.stack([row_kernels, col_kernels]), ((0, 0),) + rest)]
    concatenate x1 -> x0, other arithmetic: 0.73 us -> none  [body(): scalars = jnp.concatenate([tile_patch, jnp.stack(sides).astype(jnp.int32)])]
    pallas_call x4 -> x7, Pallas kernels: 17.8 us -> 17.3 us  [the longest x3 9.49 us: body(): pl.pallas_call(functools.partial(back, dims), in_specs=[hbm] + [whole] *...]
  transfers between devices with their start and end apart: 8 -> 8, of which waited for: 3 -> 3; matrix products, arithmetic and copies ran while one was open for 7% -> 0% of each run, Pallas kernels for 31% -> 36%
where the time goes in v4:
time: 34.4 us; the launch traced here: 34.2 us
  Pallas kernels  17.3 us (50%)
  starting transfers between devices  11.1 us (32%)
  waiting for transfers between devices  5.02 us (15%)
  between operations  0.74 us (2%)
    ppermute x8, starting transfers between devices, exchange(): return lax.ppermute(cells, axis, [(i, i ^ step) for i in range(count)])  11.1 us
    pallas_call x3, Pallas kernels, body(): pl.pallas_call(functools.partial(back, dims), in_specs=[hbm] + [whole] *...  9.49 us
    pallas_call x2, Pallas kernels, body(): pl.pallas_call(functools.partial(front, dims), in_specs=[hbm] + [whole] *...  5.92 us
    ppermute x8, waiting for transfers between devices, exchange(): return lax.ppermute(cells, axis, [(i, i ^ step) for i in range(count)])  5.02 us
    pallas_call x1, Pallas kernels, body(): pl.pallas_call(prep, in_specs=[hbm] * 5, out_specs=[whole] * (colours + 3...  1.23 us
  transfers between devices with their start and end apart: 8, of which 3 were waited for; matrix products, arithmetic and copies ran while one was open for 0% of the time, Pallas kernels for 36%

profile of v4, /device:TPU:0, one launch (start us, length us, event | category | flops | bytes accessed | tf_op | source)
XLA Modules:
  0.0 34.2 jit_solution(8727600851762014622)
XLA Ops:
  0.6 1.2 %prep.1 = (bf16[1,1,542,256]{3,2,1,0:T(8,128)(2,1)S(1)}, bf16[1,1,542,256]{3,2,1,0:T(8,128)(2,1)S(1)}, bf16[1,1,542,256]{3,2,1,0:T(8,128)(2,1)S(1)}, bf16[2,2,3,...) custom-call(bf16[1,3,542,256]{3,2,1,0:T(8,128)(2,1)} %pattern.1, ...), custom_call_target="tpu_custom_call" | custom-call | flops 10000000 | bytes 4000000 | tf_op jit(solution)/shard_map/prep/pallas_call | solution.py:306
  1.9 3.0 %collective-permute-start.1 = (bf16[1,1,542,256]{3,2,1,0:T(8,128)(2,1)S(1)}, bf16[1,1,542,256]{3,2,1,0:T(8,128)(2,1)S(1)}, u32[]{:S(2)}, u32[]{:S(2)}) collective-permute-start(bf16[1,1,542,256]{3,2,1,0:T(8,128)(2,1)S(1)} %get-tuple-element.17.refs_0_.w_own), channel_id=1, source_target_pairs={{0,16},{16,0},{1,17},{17,1},{2,18},{18,2},{3,19},{19,3},{4,20},{20... | collective-permute-start | bytes 832520 | tf_op jit(solution)/shard_map/ppermute | solution.py:30
  4.9 1.6 %collective-permute-start = (bf16[2,2,3,4,512]{4,3,2,1,0:T(4,128)(2,1)S(1)}, bf16[2,2,3,4,512]{4,3,2,1,0:T(4,128)(2,1)S(1)}, u32[]{:S(2)}, u32[]{:S(2)}) collective-permute-start(bf16[2,2,3,4,512]{4,3,2,1,0:T(4,128)(2,1)S(1)} %get-tuple-element.22.refs_3_), channel_id=1, source_target_pairs={{0,1},{1,0},{2,3},{3,2},{4,5},{5,4},{6,7},{7,6},{8,9},{9,8},{10,11... | collective-permute-start | bytes 147464 | tf_op jit(solution)/shard_map/ppermute | solution.py:30
  6.5 2.6 %collective-permute-start.2 = (bf16[2,2,3,4,512]{4,3,2,1,0:T(4,128)(2,1)S(1)}, bf16[2,2,3,4,512]{4,3,2,1,0:T(4,128)(2,1)S(1)}, u32[]{:S(2)}, u32[]{:S(2)}) collective-permute-start(bf16[2,2,3,4,512]{4,3,2,1,0:T(4,128)(2,1)S(1)} %get-tuple-element.22.refs_3_), channel_id=1, source_target_pairs={{0,2},{1,3},{2,0},{3,1},{4,6},{5,7},{6,4},{7,5},{8,10},{9,11},{10,... | collective-permute-start | bytes 147464 | tf_op jit(solution)/shard_map/ppermute | solution.py:30
  9.1 0.2 collective-permute-start.3
  9.3 0.3 collective-permute-start.4
  9.6 0.0 collective-permute-done.refs_4_
  9.6 1.7 %collective-permute-start.5 = (bf16[1,1,542,256]{3,2,1,0:T(8,128)(2,1)S(1)}, bf16[1,1,542,256]{3,2,1,0:T(8,128)(2,1)S(1)}, u32[]{:S(2)}, u32[]{:S(2)}) collective-permute-start(bf16[1,1,542,256]{3,2,1,0:T(8,128)(2,1)S(1)} %get-tuple-element.21.refs_2_.w_own), channel_id=1, source_target_pairs={{0,16},{16,0},{1,17},{17,1},{2,18},{18,2},{3,19},{19,3},{4,20},{20... | collective-permute-start | bytes 832520 | tf_op jit(solution)/shard_map/ppermute | solution.py:30
  11.3 3.0 %front0.1 = (bf16[3,1,2,2048,128]{4,3,2,1,0:T(8,128)(2,1)S(1)}, bf16[3,2,256,640]{3,2,1,0:T(8,128)(2,1)S(1)}, f32[3,2,32,128]{3,2,1,0:T(8,128)S(1)}, bf16[3,2,10...) custom-call(s32[2]{0:T(128)} %tile_patch.9, ...), custom_call_target="tpu_custom_call" | custom-call | flops 1000000000 | bytes 4000000 | tf_op jit(solution)/shard_map/front0/pallas_call | solution.py:357
  14.3 0.0 collective-permute-done.2.refs_3_
  14.3 0.6 %collective-permute-done.3.refs_4_ = bf16[2,2,3,4,512]{4,3,2,1,0:T(4,128)(2,1)S(1)} collective-permute-done((bf16[2,2,3,4,512]{4,3,2,1,0:T(4,128)(2,1)S(1)}, bf16[2,2,3,4,512]{4,3,2,1,0:T(4,128)(2,1)S(1)}, u32[]{:S(2)}, u32[]{:S(2)}) %collective-permute-start.3) | collective-permute-done | bytes 49184 | tf_op jit(solution)/shard_map/ppermute | solution.py:30
  15.0 2.9 %front1.1 = (bf16[3,1,2,2048,128]{4,3,2,1,0:T(8,128)(2,1)S(1)}, bf16[3,2,256,640]{3,2,1,0:T(8,128)(2,1)S(1)}, f32[3,2,32,128]{3,2,1,0:T(8,128)S(1)}) custom-call(s32[2]{0:T(128)} %tile_patch.9, s32[1,256]{1,0:T(1,128)S(1)} %get-tuple-element.19.sat, bf16[1,1,542,256]{3,2,1,0:T(8,128)(2,1)S(1)} %get-tuple-element.17.refs_0_.w_own, ...), custom_call_target="tpu_custom_call" | custom-call | flops 1000000000 | bytes 4000000 | tf_op jit(solution)/shard_map/front1/pallas_call | solution.py:357
  17.9 0.0 collective-permute-done.1.refs_0_
  17.9 3.2 %back0.1 = f32[2,2,4,512]{3,2,1,0:T(4,128)S(1)} custom-call(s32[2]{0:T(128)} %tile_patch.9, bf16[1,1,542,256]{3,2,1,0:T(8,128)(2,1)S(1)} %get-tuple-element.17.refs_0_.w_own, bf16[1,3,32,256]{3,2,1,0:T(8,128)(2,1)S(1)} %get-tuple-element.18.meas, f32[32,256]{1,0:T(8,128)S(1)} %get-tuple-element.23.keep, ...), custom_call_target="tpu_custom_call" | custom-call | flops 1000000000 | bytes 4000000 | tf_op jit(solution)/shard_map/back0/pallas_call | solution.py:381
  21.1 0.0 collective-permute-done.4.refs_0_
  21.1 3.2 %back1.1 = f32[2,2,4,512]{3,2,1,0:T(4,128)S(1)} custom-call(s32[2]{0:T(128)} %tile_patch.9, bf16[1,1,542,256]{3,2,1,0:T(8,128)(2,1)S(1)} %get-tuple-element.20.refs_1_.w_own, bf16[1,3,32,256]{3,2,1,0:T(8,128)(2,1)S(1)} %get-tuple-element.18.meas, f32[32,256]{1,0:T(8,128)S(1)} %get-tuple-element.23.keep, ...), custom_call_target="tpu_custom_call" | custom-call | flops 1000000000 | bytes 4000000 | tf_op jit(solution)/shard_map/back1/pallas_call | solution.py:381
  24.3 0.0 collective-permute-done.5.refs_0_
  24.3 3.2 %back2.1 = f32[2,2,4,512]{3,2,1,0:T(4,128)S(1)} custom-call(s32[2]{0:T(128)} %tile_patch.9, bf16[1,1,542,256]{3,2,1,0:T(8,128)(2,1)S(1)} %get-tuple-element.21.refs_2_.w_own, bf16[1,3,32,256]{3,2,1,0:T(8,128)(2,1)S(1)} %get-tuple-element.18.meas, f32[32,256]{1,0:T(8,128)S(1)} %get-tuple-element.23.keep, ...), custom_call_target="tpu_custom_call" | custom-call | flops 1000000000 | bytes 4000000 | tf_op jit(solution)/shard_map/back2/pallas_call | solution.py:381
  27.5 1.6 %collective-permute-start.6 = (f32[2,2,3,4,512]{4,3,2,1,0:T(4,128)S(1)}, f32[2,2,3,4,512]{4,3,2,1,0:T(4,128)S(1)}, u32[]{:S(2)}, u32[]{:S(2)}) collective-permute-start(f32[2,2,3,4,512]{4,3,2,1,0:T(4,128)S(1)} %pad_maximum_fusion), channel_id=1, source_target_pairs={{0,8},{4,12},{8,0},{12,4},{1,9},{5,13},{9,1},{13,5},{2,10},{6,14},... | collective-permute-start | bytes 294920 | tf_op jit(solution)/shard_map/ppermute | solution.py:30
  29.1 3.1 %collective-permute-done.6 = f32[2,2,3,4,512]{4,3,2,1,0:T(4,128)S(1)} collective-permute-done((f32[2,2,3,4,512]{4,3,2,1,0:T(4,128)S(1)}, f32[2,2,3,4,512]{4,3,2,1,0:T(4,128)S(1)}, u32[]{:S(2)}, u32[]{:S(2)}) %collective-permute-start.6) | collective-permute-done | bytes 98336 | tf_op jit(solution)/shard_map/ppermute | solution.py:30
  32.2 0.1 collective-permute-start.7
  32.3 1.3 %collective-permute-done.7.theirs = f32[2,2,3,4,512]{4,3,2,1,0:T(4,128)S(1)} collective-permute-done((f32[2,2,3,4,512]{4,3,2,1,0:T(4,128)S(1)}, f32[2,2,3,4,512]{4,3,2,1,0:T(4,128)S(1)}, u32[]{:S(2)}, u32[]{:S(2)}) %collective-permute-start.7) | collective-permute-done | bytes 98336 | tf_op jit(solution)/shard_map/ppermute | solution.py:30
  33.6 0.6 %finish.1 = (f32[2,3,4,511]{3,2,1,0:T(4,128)}, f32[2,3,4,511]{3,2,1,0:T(4,128)}) custom-call(f32[2,2,3,4,512]{4,3,2,1,0:T(4,128)S(1)} %fusion.mine, f32[2,2,3,4,512]{4,3,2,1,0:T(4,128)S(1)} %collective-permute-done.7.theirs), custom_call_target="tpu_custom_call" | custom-call | tf_op jit(solution)/shard_map/finish/pallas_call | solution.py:407
  (2 shorter events, 0.1 us)
Async XLA Ops:
  1.9 16.0 %collective-permute-start.1 = (bf16[1,1,542,256]{3,2,1,0:T(8,128)(2,1)S(1)}, bf16[1,1,542,256]{3,2,1,0:T(8,128)(2,1)S(1)}, u32[]{:S(2)}, u32[]{:S(2)}) collective-permute-start(bf16[1,1,542,256]{3,2,1,0:T(8,128)(2,1)S(1)} %get-tuple-element.17.refs_0_.w_own), channel_id=1, source_target_pairs={{0,16},{16,0},{1,17},{17,1},{2,18},{18,2},{3,19},{19,3},{4,20},{20... | collective-permute-start | bytes 832520 | tf_op jit(solution)/shard_map/ppermute | solution.py:30
  4.9 4.7 %collective-permute-start = (bf16[2,2,3,4,512]{4,3,2,1,0:T(4,128)(2,1)S(1)}, bf16[2,2,3,4,512]{4,3,2,1,0:T(4,128)(2,1)S(1)}, u32[]{:S(2)}, u32[]{:S(2)}) collective-permute-start(bf16[2,2,3,4,512]{4,3,2,1,0:T(4,128)(2,1)S(1)} %get-tuple-element.22.refs_3_), channel_id=1, source_target_pairs={{0,1},{1,0},{2,3},{3,2},{4,5},{5,4},{6,7},{7,6},{8,9},{9,8},{10,11... | collective-permute-start | bytes 147464 | tf_op jit(solution)/shard_map/ppermute | solution.py:30
  6.5 7.8 %collective-permute-start.2 = (bf16[2,2,3,4,512]{4,3,2,1,0:T(4,128)(2,1)S(1)}, bf16[2,2,3,4,512]{4,3,2,1,0:T(4,128)(2,1)S(1)}, u32[]{:S(2)}, u32[]{:S(2)}) collective-permute-start(bf16[2,2,3,4,512]{4,3,2,1,0:T(4,128)(2,1)S(1)} %get-tuple-element.22.refs_3_), channel_id=1, source_target_pairs={{0,2},{1,3},{2,0},{3,1},{4,6},{5,7},{6,4},{7,5},{8,10},{9,11},{10,... | collective-permute-start | bytes 147464 | tf_op jit(solution)/shard_map/ppermute | solution.py:30
  9.1 5.9 %collective-permute-start.3 = (bf16[2,2,3,4,512]{4,3,2,1,0:T(4,128)(2,1)S(1)}, bf16[2,2,3,4,512]{4,3,2,1,0:T(4,128)(2,1)S(1)}, u32[]{:S(2)}, u32[]{:S(2)}) collective-permute-start(bf16[2,2,3,4,512]{4,3,2,1,0:T(4,128)(2,1)S(1)} %get-tuple-element.22.refs_3_), channel_id=1, source_target_pairs={{0,3},{1,2},{2,1},{3,0},{4,7},{5,6},{6,5},{7,4},{8,11},{9,10},{10,... | collective-permute-start | bytes 147464 | tf_op jit(solution)/shard_map/ppermute | solution.py:30
  9.3 11.8 %collective-permute-start.4 = (bf16[1,1,542,256]{3,2,1,0:T(8,128)(2,1)S(1)}, bf16[1,1,542,256]{3,2,1,0:T(8,128)(2,1)S(1)}, u32[]{:S(2)}, u32[]{:S(2)}) collective-permute-start(bf16[1,1,542,256]{3,2,1,0:T(8,128)(2,1)S(1)} %get-tuple-element.20.refs_1_.w_own), channel_id=1, source_target_pairs={{0,16},{16,0},{1,17},{17,1},{2,18},{18,2},{3,19},{19,3},{4,20},{20... | collective-permute-start | bytes 832520 | tf_op jit(solution)/shard_map/ppermute | solution.py:30
  9.6 14.7 %collective-permute-start.5 = (bf16[1,1,542,256]{3,2,1,0:T(8,128)(2,1)S(1)}, bf16[1,1,542,256]{3,2,1,0:T(8,128)(2,1)S(1)}, u32[]{:S(2)}, u32[]{:S(2)}) collective-permute-start(bf16[1,1,542,256]{3,2,1,0:T(8,128)(2,1)S(1)} %get-tuple-element.21.refs_2_.w_own), channel_id=1, source_target_pairs={{0,16},{16,0},{1,17},{17,1},{2,18},{18,2},{3,19},{19,3},{4,20},{20... | collective-permute-start | bytes 832520 | tf_op jit(solution)/shard_map/ppermute | solution.py:30
  27.5 4.7 %collective-permute-start.6 = (f32[2,2,3,4,512]{4,3,2,1,0:T(4,128)S(1)}, f32[2,2,3,4,512]{4,3,2,1,0:T(4,128)S(1)}, u32[]{:S(2)}, u32[]{:S(2)}) collective-permute-start(f32[2,2,3,4,512]{4,3,2,1,0:T(4,128)S(1)} %pad_maximum_fusion), channel_id=1, source_target_pairs={{0,8},{4,12},{8,0},{12,4},{1,9},{5,13},{9,1},{13,5},{2,10},{6,14},... | collective-permute-start | bytes 294920 | tf_op jit(solution)/shard_map/ppermute | solution.py:30
  32.2 1.4 %collective-permute-start.7 = (f32[2,2,3,4,512]{4,3,2,1,0:T(4,128)S(1)}, f32[2,2,3,4,512]{4,3,2,1,0:T(4,128)S(1)}, u32[]{:S(2)}, u32[]{:S(2)}) collective-permute-start(f32[2,2,3,4,512]{4,3,2,1,0:T(4,128)S(1)} %fusion.mine), channel_id=1, source_target_pairs={{0,4},{4,0},{8,12},{12,8},{1,5},{5,1},{9,13},{13,9},{2,6},{6,2},{1... | collective-permute-start | bytes 294920 | tf_op jit(solution)/shard_map/ppermute | solution.py:30
